TPU v7x, 512 devices: a whole 4x4x16 slice. The times are simulated.
512 devices in a mesh: fr: 4 (over z_lo), py: 8 (over x, core), px: 16 (over z_hi, y).
Axes of the slice: x: 4, y: 4, z: 16 (z_hi: 4, z_lo: 4; z = z_hi * 4 + z_lo), core: 2. Of those that a mesh axis runs over, the one named last changes fastest.
Arguments:
- recording: bfloat16 [640, 512, 2048], P('fr', 'py', 'px'), may hold values from -9 to 9
- shifts: int32 [640, 2], P('fr'), may hold values from -32 to 32, as said below
- components: bfloat16 [640, 256], P('fr'), may hold values from -0.3125 to 0.3125
Outputs:
- projection: bfloat16 [256, 512, 2048], P('fr', 'py', 'px')
Inputs may be any that keep to these rules, and one draw needn't show every extreme that they name: `shifts`: some frame has row shift 32 and some frame has column shift -32.
All inputs are finite; a program needn't handle non-finite values.
Results may differ from a plain program's by a relative error of at most 0.014.
Values may be sent and summed in bfloat16 or wider, within the bound.
A program may use at most 64 MiB of HBM per device.

v0:
```python
import jax
import jax.numpy as jnp
from jax import lax
from jax.sharding import PartitionSpec as P

SHIFT_MAX = 32
RADIUS = 4
FRAME_BLOCK = 32


def padded_2(cells, sides, width):
    for axis, dim in sides:
        count = lax.axis_size(axis)
        ends = count - 1
        head = lax.slice_in_dim(cells, 0, width, axis=dim)
        tail = lax.slice_in_dim(cells, cells.shape[dim] - width, cells.shape[dim], axis=dim)
        cells = jnp.concatenate(
            [
                lax.ppermute(tail, axis, [(i, (i + 1) % count) for i in range(ends)]),
                cells,
                lax.ppermute(head, axis, [((i + 1) % count, i) for i in range(ends)]),
            ],
            axis=dim,
        )
    return cells


def band_matrix(out_size, radius):
    in_size = out_size + 2 * radius
    out_index = lax.broadcasted_iota(jnp.int32, (out_size, in_size), 0)
    in_index = lax.broadcasted_iota(jnp.int32, (out_size, in_size), 1)
    offset = in_index - out_index - radius
    inside = (offset >= -radius) & (offset <= radius)
    weight = jnp.float32(1.0 / (2 * radius + 1))
    return jnp.where(inside, weight, jnp.float32(0.0)).astype(jnp.bfloat16)


def select_table(starts, out_size, in_size):
    out_index = lax.broadcasted_iota(jnp.int32, (starts.shape[0], out_size, in_size), 1)
    in_index = lax.broadcasted_iota(jnp.int32, (starts.shape[0], out_size, in_size), 2)
    return (in_index == out_index + starts[:, None, None]).astype(jnp.bfloat16)


def cut_window(padded, shift_block, win_rows, win_cols):
    row_table = select_table(SHIFT_MAX - shift_block[:, 0], win_rows, padded.shape[1])
    col_table = select_table(SHIFT_MAX - shift_block[:, 1], win_cols, padded.shape[2])
    picked_rows = jnp.einsum(
        "fim,fmn->fin", row_table, padded, preferred_element_type=jnp.float32
    ).astype(jnp.bfloat16)
    return jnp.einsum(
        "fin,fjn->fij", picked_rows, col_table, preferred_element_type=jnp.float32
    ).astype(jnp.bfloat16)


def filter_block(window, row_band, col_band):
    out_rows = row_band.shape[0]
    out_cols = col_band.shape[0]
    rows_low = jnp.einsum(
        "im,fmn->fin", row_band, window, preferred_element_type=jnp.float32
    ).astype(jnp.bfloat16)
    lowpass = jnp.einsum("fin,jn->fij", rows_low, col_band, preferred_element_type=jnp.float32)
    central = window[:, RADIUS : RADIUS + out_rows, RADIUS : RADIUS + out_cols].astype(jnp.float32)
    return (central - lowpass).astype(jnp.bfloat16)


def body(recording, shifts, components):
    frames, tile_rows, tile_cols = recording.shape
    col_band = band_matrix(tile_cols, RADIUS)
    blocks = frames // FRAME_BLOCK
    row_band = band_matrix(tile_rows, RADIUS)

    def advance(counter, inputs):
        raw_block, shift_block = inputs
        padded = padded_2(raw_block, (("py", 1), ("px", 2)), SHIFT_MAX)
        registered = cut_window(padded, shift_block, tile_rows, tile_cols)
        window = padded_2(registered, (("py", 1), ("px", 2)), RADIUS)
        return (counter, filter_block(window, row_band, col_band))

    raw_blocks = recording.reshape(blocks, FRAME_BLOCK, tile_rows, tile_cols)
    shift_blocks = shifts.reshape(blocks, FRAME_BLOCK, 2)
    counter, filtered = lax.scan(advance, jnp.int32(0), (raw_blocks, shift_blocks))
    flattened = filtered.reshape(frames, tile_rows * tile_cols)
    summed = lax.psum_scatter(
        lax.dot_general(
            components, flattened, (((0,), (0,)), ((), ())), preferred_element_type=jnp.float32
        ).astype(jnp.bfloat16),
        "fr",
        scatter_dimension=0,
        tiled=True,
    )
    return summed.reshape(-1, tile_rows, tile_cols)


def solution(mesh):
    placed = (P("fr", "py", "px"), P("fr", None), P("fr", None))
    return jax.shard_map(
        body, mesh=mesh, in_specs=placed, out_specs=P("fr", "py", "px"), check_vma=False
    )
```

profile of v0, /device:TPU:1, one launch (start us, length us, event | category | flops | bytes accessed | tf_op | source)
XLA Modules:
  0.0 510.7 jit_solution(12316878466940801421)
XLA Ops:
  6.5 5.9 %copy.24 = bf16[160,64,128]{1,2,0:T(8,128)(2,1)} copy(bf16[160,64,128]{2,1,0:T(8,128)(2,1)} %param.5) | data formatting | bytes 5242880 | tf_op args[0]
  12.6 342.7 %while.11 = (s32[]{:T(128)}, bf16[5,32,64,128]{3,2,1,0:T(8,128)(2,1)}, s32[5,32,2]{1,0,2:T(8,128)S(1)}, bf16[5,32,64,128]{2,3,1,0:T(8,128)(2,1)}, s32[]{:T(128)}) while((s32[]{:T(128)}, bf16[5,32,64,128]{3,2,1,0:T(8,128)(2,1)}, s32[5,32,2]{1,0,2:T(8,128)S(1)}, bf16[5,32,64,128]{2,3,1,0:T(8,128)(2,1)}, s32[]{:T(128)}) %tuple.44), condition=%wide.region_1.2_spmd.clone, body=%wide.region_0.1_spmd.clone.sunk | while | flops 331049536 | bytes 21014244 | solution.py:81
  14.7 8.7 %collective-permute-start = (bf16[32,32,128]{2,1,0:T(8,128)(2,1)S(1)}, bf16[32,32,128]{2,1,0:T(8,128)(2,1)S(1)}, u32[]{:S(2)}, u32[]{:S(2)}) collective-permute-start(bf16[32,32,128]{2,1,0:T(8,128)(2,1)S(1)} %copy.44), channel_id=1, source_target_pairs={{16,0},{32,16},{48,32},{64,48},{80,64},{96,80},{112,96},{17,1},{33... | collective-permute-start | bytes 786440 | tf_op jit(solution)/shard_map/while/body/eval_jaxpr/ppermute | solution.py:21
  23.8 1.9 collective-permute-start.1
  26.2 2.8 collective-permute-done.1
  29.0 1.4 copy.47
  32.2 4.0 collective-permute-start.3
  36.3 3.5 collective-permute-done.2
  39.8 1.8 collective-permute-done.3
  42.3 3.9 fusion.104
  47.1 1.9 collective-permute-start.4
  49.0 3.6 collective-permute-start.5
  57.1 4.7 collective-permute-start.7
  63.2 2.2 fusion.107
  67.5 1.9 collective-permute-start
  69.8 5.1 collective-permute-start.1
  74.9 1.8 collective-permute-done
  78.2 1.4 copy.47
  81.4 4.6 collective-permute-start.3
  86.0 1.8 collective-permute-done.2
  87.8 1.5 collective-permute-done.3
  90.0 3.9 fusion.104
  94.8 1.9 collective-permute-start.4
  96.7 5.3 %collective-permute-start.5 = (bf16[32,4,128]{2,1,0:T(4,128)(2,1)S(1)}, bf16[32,4,128]{2,1,0:T(4,128)(2,1)S(1)}, u32[]{:S(2)}, u32[]{:S(2)}) collective-permute-start(bf16[32,4,128]{2,1,0:T(4,128)(2,1)S(1)} %get-tuple-element.121), channel_id=1, source_target_pairs={{0,16},{16,32},{32,48},{48,64},{64,80},{80,96},{96,112},{1,17},{17... | collective-permute-start | bytes 98312 | tf_op jit(solution)/shard_map/while/body/eval_jaxpr/ppermute | solution.py:19
  106.6 21.5 %collective-permute-start.7 = (bf16[32,72,4]{1,0,2:T(8,128)(2,1)S(1)}, bf16[32,72,4]{1,0,2:T(8,128)(2,1)S(1)}, u32[]{:S(2)}, u32[]{:S(2)}) collective-permute-start(bf16[32,72,4]{1,0,2:T(8,128)(2,1)S(1)} %copy.50), channel_id=1, source_target_pairs={{0,1},{1,2},{2,3},{3,4},{4,5},{5,6},{6,7},{7,8},{8,9},{9,10},{10,1... | collective-permute-start | bytes 55304 | tf_op jit(solution)/shard_map/while/body/eval_jaxpr/ppermute | solution.py:19
  129.4 2.1 fusion.107
  133.7 1.9 collective-permute-start
  135.9 5.1 collective-permute-start.1
  141.0 1.8 collective-permute-done
  147.6 10.3 %collective-permute-start.3 = (bf16[32,128,32]{1,2,0:T(8,128)(2,1)S(1)}, bf16[32,128,32]{1,2,0:T(8,128)(2,1)S(1)}, u32[]{:S(2)}, u32[]{:S(2)}) collective-permute-start(bf16[32,128,32]{1,2,0:T(8,128)(2,1)S(1)} %get-tuple-element.118), channel_id=1, source_target_pairs={{0,1},{1,2},{2,3},{3,4},{4,5},{5,6},{6,7},{7,8},{8,9},{9,10},{10,1... | collective-permute-start | bytes 786440 | tf_op jit(solution)/shard_map/while/body/eval_jaxpr/ppermute | solution.py:19
  157.9 1.8 collective-permute-done.2
  159.7 1.5 collective-permute-done.3
  161.9 3.9 fusion.104
  166.7 1.9 collective-permute-start.4
  168.6 5.4 %collective-permute-start.5 = (bf16[32,4,128]{2,1,0:T(4,128)(2,1)S(1)}, bf16[32,4,128]{2,1,0:T(4,128)(2,1)S(1)}, u32[]{:S(2)}, u32[]{:S(2)}) collective-permute-start(bf16[32,4,128]{2,1,0:T(4,128)(2,1)S(1)} %get-tuple-element.121), channel_id=1, source_target_pairs={{0,16},{16,32},{32,48},{48,64},{64,80},{80,96},{96,112},{1,17},{17... | collective-permute-start | bytes 98312 | tf_op jit(solution)/shard_map/while/body/eval_jaxpr/ppermute | solution.py:19
  178.5 25.4 %collective-permute-start.7 = (bf16[32,72,4]{1,0,2:T(8,128)(2,1)S(1)}, bf16[32,72,4]{1,0,2:T(8,128)(2,1)S(1)}, u32[]{:S(2)}, u32[]{:S(2)}) collective-permute-start(bf16[32,72,4]{1,0,2:T(8,128)(2,1)S(1)} %copy.50), channel_id=1, source_target_pairs={{0,1},{1,2},{2,3},{3,4},{4,5},{5,6},{6,7},{7,8},{8,9},{9,10},{10,1... | collective-permute-start | bytes 55304 | tf_op jit(solution)/shard_map/while/body/eval_jaxpr/ppermute | solution.py:19
  205.2 2.1 fusion.107
  209.5 1.9 collective-permute-start
  211.8 5.1 collective-permute-start.1
  216.9 1.8 collective-permute-done
  223.4 10.3 %collective-permute-start.3 = (bf16[32,128,32]{1,2,0:T(8,128)(2,1)S(1)}, bf16[32,128,32]{1,2,0:T(8,128)(2,1)S(1)}, u32[]{:S(2)}, u32[]{:S(2)}) collective-permute-start(bf16[32,128,32]{1,2,0:T(8,128)(2,1)S(1)} %get-tuple-element.118), channel_id=1, source_target_pairs={{0,1},{1,2},{2,3},{3,4},{4,5},{5,6},{6,7},{7,8},{8,9},{9,10},{10,1... | collective-permute-start | bytes 786440 | tf_op jit(solution)/shard_map/while/body/eval_jaxpr/ppermute | solution.py:19
  233.7 1.8 collective-permute-done.2
  235.5 1.5 collective-permute-done.3
  237.7 3.9 fusion.104
  242.5 1.9 collective-permute-start.4
  244.4 5.5 %collective-permute-start.5 = (bf16[32,4,128]{2,1,0:T(4,128)(2,1)S(1)}, bf16[32,4,128]{2,1,0:T(4,128)(2,1)S(1)}, u32[]{:S(2)}, u32[]{:S(2)}) collective-permute-start(bf16[32,4,128]{2,1,0:T(4,128)(2,1)S(1)} %get-tuple-element.121), channel_id=1, source_target_pairs={{0,16},{16,32},{32,48},{48,64},{64,80},{80,96},{96,112},{1,17},{17... | collective-permute-start | bytes 98312 | tf_op jit(solution)/shard_map/while/body/eval_jaxpr/ppermute | solution.py:19
  254.5 23.5 %collective-permute-start.7 = (bf16[32,72,4]{1,0,2:T(8,128)(2,1)S(1)}, bf16[32,72,4]{1,0,2:T(8,128)(2,1)S(1)}, u32[]{:S(2)}, u32[]{:S(2)}) collective-permute-start(bf16[32,72,4]{1,0,2:T(8,128)(2,1)S(1)} %copy.50), channel_id=1, source_target_pairs={{0,1},{1,2},{2,3},{3,4},{4,5},{5,6},{6,7},{7,8},{8,9},{9,10},{10,1... | collective-permute-start | bytes 55304 | tf_op jit(solution)/shard_map/while/body/eval_jaxpr/ppermute | solution.py:19
  279.3 2.1 fusion.107
  283.6 1.9 collective-permute-start
  285.8 5.1 collective-permute-start.1
  290.9 1.8 collective-permute-done
  297.4 10.3 %collective-permute-start.3 = (bf16[32,128,32]{1,2,0:T(8,128)(2,1)S(1)}, bf16[32,128,32]{1,2,0:T(8,128)(2,1)S(1)}, u32[]{:S(2)}, u32[]{:S(2)}) collective-permute-start(bf16[32,128,32]{1,2,0:T(8,128)(2,1)S(1)} %get-tuple-element.118), channel_id=1, source_target_pairs={{0,1},{1,2},{2,3},{3,4},{4,5},{5,6},{6,7},{7,8},{8,9},{9,10},{10,1... | collective-permute-start | bytes 786440 | tf_op jit(solution)/shard_map/while/body/eval_jaxpr/ppermute | solution.py:19
  307.8 1.8 collective-permute-done.2
  309.6 1.5 collective-permute-done.3
  311.8 3.9 fusion.104
  316.6 1.9 collective-permute-start.4
  318.5 5.4 %collective-permute-start.5 = (bf16[32,4,128]{2,1,0:T(4,128)(2,1)S(1)}, bf16[32,4,128]{2,1,0:T(4,128)(2,1)S(1)}, u32[]{:S(2)}, u32[]{:S(2)}) collective-permute-start(bf16[32,4,128]{2,1,0:T(4,128)(2,1)S(1)} %get-tuple-element.121), channel_id=1, source_target_pairs={{0,16},{16,32},{32,48},{48,64},{64,80},{80,96},{96,112},{1,17},{17... | collective-permute-start | bytes 98312 | tf_op jit(solution)/shard_map/while/body/eval_jaxpr/ppermute | solution.py:19
  328.4 23.4 %collective-permute-start.7 = (bf16[32,72,4]{1,0,2:T(8,128)(2,1)S(1)}, bf16[32,72,4]{1,0,2:T(8,128)(2,1)S(1)}, u32[]{:S(2)}, u32[]{:S(2)}) collective-permute-start(bf16[32,72,4]{1,0,2:T(8,128)(2,1)S(1)} %copy.50), channel_id=1, source_target_pairs={{0,1},{1,2},{2,3},{3,4},{4,5},{5,6},{6,7},{7,8},{8,9},{9,10},{10,1... | collective-permute-start | bytes 55304 | tf_op jit(solution)/shard_map/while/body/eval_jaxpr/ppermute | solution.py:19
  353.2 2.1 fusion.107
  355.3 7.5 %fusion.83 = bf16[256,8192]{0,1:T(8,128)(2,1)} fusion(bf16[160,256]{1,0:T(8,128)(2,1)S(1)} %copy-done, bf16[20,8,64,128]{3,2,1,0:T(8,128)(2,1)} %bitcast.62), kind=kOutput, calls=%fused_computation.70 | convolution fusion | flops 673185792 | bytes 6897664 | tf_op jit(solution)/shard_map/dot_general | solution.py:84
  362.8 6.4 %copy.28 = bf16[256,8192]{1,0:T(8,128)(2,1)} copy(bf16[256,8192]{0,1:T(8,128)(2,1)} %fusion.83) | data formatting | bytes 8388608
  369.2 130.3 %reduce-scatter.4.cloned.1.call-done = bf16[64,8192]{1,0:T(8,128)(2,1)} async-done(((bf16[256,8192]{1,0:T(8,128)(2,1)}), bf16[64,8192]{1,0:T(8,128)(2,1)}) %reduce-scatter.4.cloned.1.call-update) | async-done | bytes 1048592
  499.5 2.0 copy.29
  501.6 2.3 copy.26
  (151 shorter events, 69.5 us)
Async XLA Ops:
  6.5 348.8 %copy-start = (bf16[160,256]{1,0:T(8,128)(2,1)S(1)}, bf16[160,256]{1,0:T(8,128)(2,1)}, u32[]{:S(2)}) copy-start(bf16[160,256]{1,0:T(8,128)(2,1)} %param.7) | copy-start | bytes 245764
  6.5 493.0 %reduce-scatter.4.cloned.1.call-start = ((), (), s32[]{:S(2)}) async-start(), calls=%async_computation.1 | async-start | bytes 5242880
  6.5 5.9 %copy-start.2 = (s32[160,2]{0,1:T(2,128)S(1)}, s32[160,2]{0,1:T(2,128)}, u32[]{:S(2)}) copy-start(s32[160,2]{0,1:T(2,128)} %param.6) | copy-start | bytes 3844
  14.7 11.0 %collective-permute-start = (bf16[32,32,128]{2,1,0:T(8,128)(2,1)S(1)}, bf16[32,32,128]{2,1,0:T(8,128)(2,1)S(1)}, u32[]{:S(2)}, u32[]{:S(2)}) collective-permute-start(bf16[32,32,128]{2,1,0:T(8,128)(2,1)S(1)} %copy.44), channel_id=1, source_target_pairs={{16,0},{32,16},{48,32},{64,48},{80,64},{96,80},{112,96},{17,1},{33... | collective-permute-start | bytes 786440 | tf_op jit(solution)/shard_map/while/body/eval_jaxpr/ppermute | solution.py:21
  23.8 5.2 %collective-permute-start.1 = (bf16[32,32,128]{2,1,0:T(8,128)(2,1)S(1)}, bf16[32,32,128]{2,1,0:T(8,128)(2,1)}, u32[]{:S(2)}, u32[]{:S(2)}) collective-permute-start(bf16[32,32,128]{2,1,0:T(8,128)(2,1)S(1)} %copy.46), channel_id=1, source_target_pairs={{0,16},{16,32},{32,48},{48,64},{64,80},{80,96},{96,112},{1,17},{17... | collective-permute-start | bytes 786440 | tf_op jit(solution)/shard_map/while/body/eval_jaxpr/ppermute | solution.py:19
  30.9 8.9 %collective-permute-start.2 = (bf16[32,128,32]{1,2,0:T(8,128)(2,1)S(1)}, bf16[32,128,32]{1,2,0:T(8,128)(2,1)S(1)}, u32[]{:S(2)}, u32[]{:S(2)}) collective-permute-start(bf16[32,128,32]{1,2,0:T(8,128)(2,1)S(1)} %get-tuple-element.117), channel_id=1, source_target_pairs={{1,0},{2,1},{3,2},{4,3},{5,4},{6,5},{7,6},{8,7},{9,8},{10,9},{11,1... | collective-permute-start | bytes 786440 | tf_op jit(solution)/shard_map/while/body/eval_jaxpr/ppermute | solution.py:21
  32.2 9.3 %collective-permute-start.3 = (bf16[32,128,32]{1,2,0:T(8,128)(2,1)S(1)}, bf16[32,128,32]{1,2,0:T(8,128)(2,1)S(1)}, u32[]{:S(2)}, u32[]{:S(2)}) collective-permute-start(bf16[32,128,32]{1,2,0:T(8,128)(2,1)S(1)} %get-tuple-element.118), channel_id=1, source_target_pairs={{0,1},{1,2},{2,3},{3,4},{4,5},{5,6},{6,7},{7,8},{8,9},{9,10},{10,1... | collective-permute-start | bytes 786440 | tf_op jit(solution)/shard_map/while/body/eval_jaxpr/ppermute | solution.py:19
  39.8 1.8 copy-start.3
  41.6 0.7 copy-start.4
  47.1 5.6 %collective-permute-start.4 = (bf16[32,4,128]{2,1,0:T(4,128)(2,1)S(1)}, bf16[32,4,128]{2,1,0:T(4,128)(2,1)S(1)}, u32[]{:S(2)}, u32[]{:S(2)}) collective-permute-start(bf16[32,4,128]{2,1,0:T(4,128)(2,1)S(1)} %get-tuple-element.120), channel_id=1, source_target_pairs={{16,0},{32,16},{48,32},{64,48},{80,64},{96,80},{112,96},{17,1},{33... | collective-permute-start | bytes 98312 | tf_op jit(solution)/shard_map/while/body/eval_jaxpr/ppermute | solution.py:21
  49.0 4.7 collective-permute-start.5
  55.0 8.2 %copy-start.1 = (bf16[32,64,128]{2,1,0:T(8,128)(2,1)S(1)}, bf16[32,64,128]{2,1,0:T(8,128)(2,1)}, u32[]{:S(2)}) copy-start(bf16[32,64,128]{2,1,0:T(8,128)(2,1)} %fusion.104) | copy-start | bytes 1572868 | tf_op jit(solution)/shard_map/while
  55.5 6.3 %collective-permute-start.6 = (bf16[32,72,4]{1,0,2:T(8,128)(2,1)S(1)}, bf16[32,72,4]{1,0,2:T(8,128)(2,1)S(1)}, u32[]{:S(2)}, u32[]{:S(2)}) collective-permute-start(bf16[32,72,4]{1,0,2:T(8,128)(2,1)S(1)} %copy.48), channel_id=1, source_target_pairs={{1,0},{2,1},{3,2},{4,3},{5,4},{6,5},{7,6},{8,7},{9,8},{10,9},{11,1... | collective-permute-start | bytes 55304 | tf_op jit(solution)/shard_map/while/body/eval_jaxpr/ppermute | solution.py:21
  57.1 5.7 %collective-permute-start.7 = (bf16[32,72,4]{1,0,2:T(8,128)(2,1)S(1)}, bf16[32,72,4]{1,0,2:T(8,128)(2,1)S(1)}, u32[]{:S(2)}, u32[]{:S(2)}) collective-permute-start(bf16[32,72,4]{1,0,2:T(8,128)(2,1)S(1)} %copy.50), channel_id=1, source_target_pairs={{0,1},{1,2},{2,3},{3,4},{4,5},{5,6},{6,7},{7,8},{8,9},{9,10},{10,1... | collective-permute-start | bytes 55304 | tf_op jit(solution)/shard_map/while/body/eval_jaxpr/ppermute | solution.py:19
  67.5 9.1 %collective-permute-start = (bf16[32,32,128]{2,1,0:T(8,128)(2,1)S(1)}, bf16[32,32,128]{2,1,0:T(8,128)(2,1)S(1)}, u32[]{:S(2)}, u32[]{:S(2)}) collective-permute-start(bf16[32,32,128]{2,1,0:T(8,128)(2,1)S(1)} %copy.44), channel_id=1, source_target_pairs={{16,0},{32,16},{48,32},{64,48},{80,64},{96,80},{112,96},{17,1},{33... | collective-permute-start | bytes 786440 | tf_op jit(solution)/shard_map/while/body/eval_jaxpr/ppermute | solution.py:21
  69.8 8.4 %collective-permute-start.1 = (bf16[32,32,128]{2,1,0:T(8,128)(2,1)S(1)}, bf16[32,32,128]{2,1,0:T(8,128)(2,1)}, u32[]{:S(2)}, u32[]{:S(2)}) collective-permute-start(bf16[32,32,128]{2,1,0:T(8,128)(2,1)S(1)} %copy.46), channel_id=1, source_target_pairs={{0,16},{16,32},{32,48},{48,64},{64,80},{80,96},{96,112},{1,17},{17... | collective-permute-start | bytes 786440 | tf_op jit(solution)/shard_map/while/body/eval_jaxpr/ppermute | solution.py:19
  80.1 7.7 %collective-permute-start.2 = (bf16[32,128,32]{1,2,0:T(8,128)(2,1)S(1)}, bf16[32,128,32]{1,2,0:T(8,128)(2,1)S(1)}, u32[]{:S(2)}, u32[]{:S(2)}) collective-permute-start(bf16[32,128,32]{1,2,0:T(8,128)(2,1)S(1)} %get-tuple-element.117), channel_id=1, source_target_pairs={{1,0},{2,1},{3,2},{4,3},{5,4},{6,5},{7,6},{8,7},{9,8},{10,9},{11,1... | collective-permute-start | bytes 786440 | tf_op jit(solution)/shard_map/while/body/eval_jaxpr/ppermute | solution.py:21
  81.4 7.9 %collective-permute-start.3 = (bf16[32,128,32]{1,2,0:T(8,128)(2,1)S(1)}, bf16[32,128,32]{1,2,0:T(8,128)(2,1)S(1)}, u32[]{:S(2)}, u32[]{:S(2)}) collective-permute-start(bf16[32,128,32]{1,2,0:T(8,128)(2,1)S(1)} %get-tuple-element.118), channel_id=1, source_target_pairs={{0,1},{1,2},{2,3},{3,4},{4,5},{5,6},{6,7},{7,8},{8,9},{9,10},{10,1... | collective-permute-start | bytes 786440 | tf_op jit(solution)/shard_map/while/body/eval_jaxpr/ppermute | solution.py:19
  87.8 1.5 copy-start.3
  89.3 0.7 copy-start.4
  94.8 7.3 %collective-permute-start.4 = (bf16[32,4,128]{2,1,0:T(4,128)(2,1)S(1)}, bf16[32,4,128]{2,1,0:T(4,128)(2,1)S(1)}, u32[]{:S(2)}, u32[]{:S(2)}) collective-permute-start(bf16[32,4,128]{2,1,0:T(4,128)(2,1)S(1)} %get-tuple-element.120), channel_id=1, source_target_pairs={{16,0},{32,16},{48,32},{64,48},{80,64},{96,80},{112,96},{17,1},{33... | collective-permute-start | bytes 98312 | tf_op jit(solution)/shard_map/while/body/eval_jaxpr/ppermute | solution.py:21
  96.7 6.4 %collective-permute-start.5 = (bf16[32,4,128]{2,1,0:T(4,128)(2,1)S(1)}, bf16[32,4,128]{2,1,0:T(4,128)(2,1)S(1)}, u32[]{:S(2)}, u32[]{:S(2)}) collective-permute-start(bf16[32,4,128]{2,1,0:T(4,128)(2,1)S(1)} %get-tuple-element.121), channel_id=1, source_target_pairs={{0,16},{16,32},{32,48},{48,64},{64,80},{80,96},{96,112},{1,17},{17... | collective-permute-start | bytes 98312 | tf_op jit(solution)/shard_map/while/body/eval_jaxpr/ppermute | solution.py:19
  104.4 25.0 %copy-start.1 = (bf16[32,64,128]{2,1,0:T(8,128)(2,1)S(1)}, bf16[32,64,128]{2,1,0:T(8,128)(2,1)}, u32[]{:S(2)}) copy-start(bf16[32,64,128]{2,1,0:T(8,128)(2,1)} %fusion.104) | copy-start | bytes 1572868 | tf_op jit(solution)/shard_map/while
  104.9 23.1 %collective-permute-start.6 = (bf16[32,72,4]{1,0,2:T(8,128)(2,1)S(1)}, bf16[32,72,4]{1,0,2:T(8,128)(2,1)S(1)}, u32[]{:S(2)}, u32[]{:S(2)}) collective-permute-start(bf16[32,72,4]{1,0,2:T(8,128)(2,1)S(1)} %copy.48), channel_id=1, source_target_pairs={{1,0},{2,1},{3,2},{4,3},{5,4},{6,5},{7,6},{8,7},{9,8},{10,9},{11,1... | collective-permute-start | bytes 55304 | tf_op jit(solution)/shard_map/while/body/eval_jaxpr/ppermute | solution.py:21
  106.6 22.5 %collective-permute-start.7 = (bf16[32,72,4]{1,0,2:T(8,128)(2,1)S(1)}, bf16[32,72,4]{1,0,2:T(8,128)(2,1)S(1)}, u32[]{:S(2)}, u32[]{:S(2)}) collective-permute-start(bf16[32,72,4]{1,0,2:T(8,128)(2,1)S(1)} %copy.50), channel_id=1, source_target_pairs={{0,1},{1,2},{2,3},{3,4},{4,5},{5,6},{6,7},{7,8},{8,9},{9,10},{10,1... | collective-permute-start | bytes 55304 | tf_op jit(solution)/shard_map/while/body/eval_jaxpr/ppermute | solution.py:19
  133.7 9.1 %collective-permute-start = (bf16[32,32,128]{2,1,0:T(8,128)(2,1)S(1)}, bf16[32,32,128]{2,1,0:T(8,128)(2,1)S(1)}, u32[]{:S(2)}, u32[]{:S(2)}) collective-permute-start(bf16[32,32,128]{2,1,0:T(8,128)(2,1)S(1)} %copy.44), channel_id=1, source_target_pairs={{16,0},{32,16},{48,32},{64,48},{80,64},{96,80},{112,96},{17,1},{33... | collective-permute-start | bytes 786440 | tf_op jit(solution)/shard_map/while/body/eval_jaxpr/ppermute | solution.py:21
  135.9 8.4 %collective-permute-start.1 = (bf16[32,32,128]{2,1,0:T(8,128)(2,1)S(1)}, bf16[32,32,128]{2,1,0:T(8,128)(2,1)}, u32[]{:S(2)}, u32[]{:S(2)}) collective-permute-start(bf16[32,32,128]{2,1,0:T(8,128)(2,1)S(1)} %copy.46), channel_id=1, source_target_pairs={{0,16},{16,32},{32,48},{48,64},{64,80},{80,96},{96,112},{1,17},{17... | collective-permute-start | bytes 786440 | tf_op jit(solution)/shard_map/while/body/eval_jaxpr/ppermute | solution.py:19
  146.3 13.4 %collective-permute-start.2 = (bf16[32,128,32]{1,2,0:T(8,128)(2,1)S(1)}, bf16[32,128,32]{1,2,0:T(8,128)(2,1)S(1)}, u32[]{:S(2)}, u32[]{:S(2)}) collective-permute-start(bf16[32,128,32]{1,2,0:T(8,128)(2,1)S(1)} %get-tuple-element.117), channel_id=1, source_target_pairs={{1,0},{2,1},{3,2},{4,3},{5,4},{6,5},{7,6},{8,7},{9,8},{10,9},{11,1... | collective-permute-start | bytes 786440 | tf_op jit(solution)/shard_map/while/body/eval_jaxpr/ppermute | solution.py:21
  147.6 13.6 %collective-permute-start.3 = (bf16[32,128,32]{1,2,0:T(8,128)(2,1)S(1)}, bf16[32,128,32]{1,2,0:T(8,128)(2,1)S(1)}, u32[]{:S(2)}, u32[]{:S(2)}) collective-permute-start(bf16[32,128,32]{1,2,0:T(8,128)(2,1)S(1)} %get-tuple-element.118), channel_id=1, source_target_pairs={{0,1},{1,2},{2,3},{3,4},{4,5},{5,6},{6,7},{7,8},{8,9},{9,10},{10,1... | collective-permute-start | bytes 786440 | tf_op jit(solution)/shard_map/while/body/eval_jaxpr/ppermute | solution.py:19
  159.7 1.5 copy-start.3
  161.2 0.7 copy-start.4
  166.7 7.3 %collective-permute-start.4 = (bf16[32,4,128]{2,1,0:T(4,128)(2,1)S(1)}, bf16[32,4,128]{2,1,0:T(4,128)(2,1)S(1)}, u32[]{:S(2)}, u32[]{:S(2)}) collective-permute-start(bf16[32,4,128]{2,1,0:T(4,128)(2,1)S(1)} %get-tuple-element.120), channel_id=1, source_target_pairs={{16,0},{32,16},{48,32},{64,48},{80,64},{96,80},{112,96},{17,1},{33... | collective-permute-start | bytes 98312 | tf_op jit(solution)/shard_map/while/body/eval_jaxpr/ppermute | solution.py:21
  168.6 6.4 %collective-permute-start.5 = (bf16[32,4,128]{2,1,0:T(4,128)(2,1)S(1)}, bf16[32,4,128]{2,1,0:T(4,128)(2,1)S(1)}, u32[]{:S(2)}, u32[]{:S(2)}) collective-permute-start(bf16[32,4,128]{2,1,0:T(4,128)(2,1)S(1)} %get-tuple-element.121), channel_id=1, source_target_pairs={{0,16},{16,32},{32,48},{48,64},{64,80},{80,96},{96,112},{1,17},{17... | collective-permute-start | bytes 98312 | tf_op jit(solution)/shard_map/while/body/eval_jaxpr/ppermute | solution.py:19
  176.3 28.9 %copy-start.1 = (bf16[32,64,128]{2,1,0:T(8,128)(2,1)S(1)}, bf16[32,64,128]{2,1,0:T(8,128)(2,1)}, u32[]{:S(2)}) copy-start(bf16[32,64,128]{2,1,0:T(8,128)(2,1)} %fusion.104) | copy-start | bytes 1572868 | tf_op jit(solution)/shard_map/while
  176.8 27.0 %collective-permute-start.6 = (bf16[32,72,4]{1,0,2:T(8,128)(2,1)S(1)}, bf16[32,72,4]{1,0,2:T(8,128)(2,1)S(1)}, u32[]{:S(2)}, u32[]{:S(2)}) collective-permute-start(bf16[32,72,4]{1,0,2:T(8,128)(2,1)S(1)} %copy.48), channel_id=1, source_target_pairs={{1,0},{2,1},{3,2},{4,3},{5,4},{6,5},{7,6},{8,7},{9,8},{10,9},{11,1... | collective-permute-start | bytes 55304 | tf_op jit(solution)/shard_map/while/body/eval_jaxpr/ppermute | solution.py:21
  178.5 26.4 %collective-permute-start.7 = (bf16[32,72,4]{1,0,2:T(8,128)(2,1)S(1)}, bf16[32,72,4]{1,0,2:T(8,128)(2,1)S(1)}, u32[]{:S(2)}, u32[]{:S(2)}) collective-permute-start(bf16[32,72,4]{1,0,2:T(8,128)(2,1)S(1)} %copy.50), channel_id=1, source_target_pairs={{0,1},{1,2},{2,3},{3,4},{4,5},{5,6},{6,7},{7,8},{8,9},{9,10},{10,1... | collective-permute-start | bytes 55304 | tf_op jit(solution)/shard_map/while/body/eval_jaxpr/ppermute | solution.py:19
  209.5 9.1 %collective-permute-start = (bf16[32,32,128]{2,1,0:T(8,128)(2,1)S(1)}, bf16[32,32,128]{2,1,0:T(8,128)(2,1)S(1)}, u32[]{:S(2)}, u32[]{:S(2)}) collective-permute-start(bf16[32,32,128]{2,1,0:T(8,128)(2,1)S(1)} %copy.44), channel_id=1, source_target_pairs={{16,0},{32,16},{48,32},{64,48},{80,64},{96,80},{112,96},{17,1},{33... | collective-permute-start | bytes 786440 | tf_op jit(solution)/shard_map/while/body/eval_jaxpr/ppermute | solution.py:21
  211.8 8.4 %collective-permute-start.1 = (bf16[32,32,128]{2,1,0:T(8,128)(2,1)S(1)}, bf16[32,32,128]{2,1,0:T(8,128)(2,1)}, u32[]{:S(2)}, u32[]{:S(2)}) collective-permute-start(bf16[32,32,128]{2,1,0:T(8,128)(2,1)S(1)} %copy.46), channel_id=1, source_target_pairs={{0,16},{16,32},{32,48},{48,64},{64,80},{80,96},{96,112},{1,17},{17... | collective-permute-start | bytes 786440 | tf_op jit(solution)/shard_map/while/body/eval_jaxpr/ppermute | solution.py:19
  222.1 13.4 %collective-permute-start.2 = (bf16[32,128,32]{1,2,0:T(8,128)(2,1)S(1)}, bf16[32,128,32]{1,2,0:T(8,128)(2,1)S(1)}, u32[]{:S(2)}, u32[]{:S(2)}) collective-permute-start(bf16[32,128,32]{1,2,0:T(8,128)(2,1)S(1)} %get-tuple-element.117), channel_id=1, source_target_pairs={{1,0},{2,1},{3,2},{4,3},{5,4},{6,5},{7,6},{8,7},{9,8},{10,9},{11,1... | collective-permute-start | bytes 786440 | tf_op jit(solution)/shard_map/while/body/eval_jaxpr/ppermute | solution.py:21
  223.4 13.6 %collective-permute-start.3 = (bf16[32,128,32]{1,2,0:T(8,128)(2,1)S(1)}, bf16[32,128,32]{1,2,0:T(8,128)(2,1)S(1)}, u32[]{:S(2)}, u32[]{:S(2)}) collective-permute-start(bf16[32,128,32]{1,2,0:T(8,128)(2,1)S(1)} %get-tuple-element.118), channel_id=1, source_target_pairs={{0,1},{1,2},{2,3},{3,4},{4,5},{5,6},{6,7},{7,8},{8,9},{9,10},{10,1... | collective-permute-start | bytes 786440 | tf_op jit(solution)/shard_map/while/body/eval_jaxpr/ppermute | solution.py:19
  235.5 1.5 copy-start.3
  237.0 0.7 copy-start.4
  242.5 7.5 %collective-permute-start.4 = (bf16[32,4,128]{2,1,0:T(4,128)(2,1)S(1)}, bf16[32,4,128]{2,1,0:T(4,128)(2,1)S(1)}, u32[]{:S(2)}, u32[]{:S(2)}) collective-permute-start(bf16[32,4,128]{2,1,0:T(4,128)(2,1)S(1)} %get-tuple-element.120), channel_id=1, source_target_pairs={{16,0},{32,16},{48,32},{64,48},{80,64},{96,80},{112,96},{17,1},{33... | collective-permute-start | bytes 98312 | tf_op jit(solution)/shard_map/while/body/eval_jaxpr/ppermute | solution.py:21
  244.4 6.5 %collective-permute-start.5 = (bf16[32,4,128]{2,1,0:T(4,128)(2,1)S(1)}, bf16[32,4,128]{2,1,0:T(4,128)(2,1)S(1)}, u32[]{:S(2)}, u32[]{:S(2)}) collective-permute-start(bf16[32,4,128]{2,1,0:T(4,128)(2,1)S(1)} %get-tuple-element.121), channel_id=1, source_target_pairs={{0,16},{16,32},{32,48},{48,64},{64,80},{80,96},{96,112},{1,17},{17... | collective-permute-start | bytes 98312 | tf_op jit(solution)/shard_map/while/body/eval_jaxpr/ppermute | solution.py:19
  252.3 27.0 %copy-start.1 = (bf16[32,64,128]{2,1,0:T(8,128)(2,1)S(1)}, bf16[32,64,128]{2,1,0:T(8,128)(2,1)}, u32[]{:S(2)}) copy-start(bf16[32,64,128]{2,1,0:T(8,128)(2,1)} %fusion.104) | copy-start | bytes 1572868 | tf_op jit(solution)/shard_map/while
  252.8 25.1 %collective-permute-start.6 = (bf16[32,72,4]{1,0,2:T(8,128)(2,1)S(1)}, bf16[32,72,4]{1,0,2:T(8,128)(2,1)S(1)}, u32[]{:S(2)}, u32[]{:S(2)}) collective-permute-start(bf16[32,72,4]{1,0,2:T(8,128)(2,1)S(1)} %copy.48), channel_id=1, source_target_pairs={{1,0},{2,1},{3,2},{4,3},{5,4},{6,5},{7,6},{8,7},{9,8},{10,9},{11,1... | collective-permute-start | bytes 55304 | tf_op jit(solution)/shard_map/while/body/eval_jaxpr/ppermute | solution.py:21
  254.5 24.5 %collective-permute-start.7 = (bf16[32,72,4]{1,0,2:T(8,128)(2,1)S(1)}, bf16[32,72,4]{1,0,2:T(8,128)(2,1)S(1)}, u32[]{:S(2)}, u32[]{:S(2)}) collective-permute-start(bf16[32,72,4]{1,0,2:T(8,128)(2,1)S(1)} %copy.50), channel_id=1, source_target_pairs={{0,1},{1,2},{2,3},{3,4},{4,5},{5,6},{6,7},{7,8},{8,9},{9,10},{10,1... | collective-permute-start | bytes 55304 | tf_op jit(solution)/shard_map/while/body/eval_jaxpr/ppermute | solution.py:19
  283.6 9.1 %collective-permute-start = (bf16[32,32,128]{2,1,0:T(8,128)(2,1)S(1)}, bf16[32,32,128]{2,1,0:T(8,128)(2,1)S(1)}, u32[]{:S(2)}, u32[]{:S(2)}) collective-permute-start(bf16[32,32,128]{2,1,0:T(8,128)(2,1)S(1)} %copy.44), channel_id=1, source_target_pairs={{16,0},{32,16},{48,32},{64,48},{80,64},{96,80},{112,96},{17,1},{33... | collective-permute-start | bytes 786440 | tf_op jit(solution)/shard_map/while/body/eval_jaxpr/ppermute | solution.py:21
  285.8 8.4 %collective-permute-start.1 = (bf16[32,32,128]{2,1,0:T(8,128)(2,1)S(1)}, bf16[32,32,128]{2,1,0:T(8,128)(2,1)}, u32[]{:S(2)}, u32[]{:S(2)}) collective-permute-start(bf16[32,32,128]{2,1,0:T(8,128)(2,1)S(1)} %copy.46), channel_id=1, source_target_pairs={{0,16},{16,32},{32,48},{48,64},{64,80},{80,96},{96,112},{1,17},{17... | collective-permute-start | bytes 786440 | tf_op jit(solution)/shard_map/while/body/eval_jaxpr/ppermute | solution.py:19
  296.1 13.4 %collective-permute-start.2 = (bf16[32,128,32]{1,2,0:T(8,128)(2,1)S(1)}, bf16[32,128,32]{1,2,0:T(8,128)(2,1)S(1)}, u32[]{:S(2)}, u32[]{:S(2)}) collective-permute-start(bf16[32,128,32]{1,2,0:T(8,128)(2,1)S(1)} %get-tuple-element.117), channel_id=1, source_target_pairs={{1,0},{2,1},{3,2},{4,3},{5,4},{6,5},{7,6},{8,7},{9,8},{10,9},{11,1... | collective-permute-start | bytes 786440 | tf_op jit(solution)/shard_map/while/body/eval_jaxpr/ppermute | solution.py:21
  297.4 13.6 %collective-permute-start.3 = (bf16[32,128,32]{1,2,0:T(8,128)(2,1)S(1)}, bf16[32,128,32]{1,2,0:T(8,128)(2,1)S(1)}, u32[]{:S(2)}, u32[]{:S(2)}) collective-permute-start(bf16[32,128,32]{1,2,0:T(8,128)(2,1)S(1)} %get-tuple-element.118), channel_id=1, source_target_pairs={{0,1},{1,2},{2,3},{3,4},{4,5},{5,6},{6,7},{7,8},{8,9},{9,10},{10,1... | collective-permute-start | bytes 786440 | tf_op jit(solution)/shard_map/while/body/eval_jaxpr/ppermute | solution.py:19
  309.6 1.5 copy-start.3
  311.0 0.7 copy-start.4
  316.6 7.3 %collective-permute-start.4 = (bf16[32,4,128]{2,1,0:T(4,128)(2,1)S(1)}, bf16[32,4,128]{2,1,0:T(4,128)(2,1)S(1)}, u32[]{:S(2)}, u32[]{:S(2)}) collective-permute-start(bf16[32,4,128]{2,1,0:T(4,128)(2,1)S(1)} %get-tuple-element.120), channel_id=1, source_target_pairs={{16,0},{32,16},{48,32},{64,48},{80,64},{96,80},{112,96},{17,1},{33... | collective-permute-start | bytes 98312 | tf_op jit(solution)/shard_map/while/body/eval_jaxpr/ppermute | solution.py:21
  318.5 6.4 %collective-permute-start.5 = (bf16[32,4,128]{2,1,0:T(4,128)(2,1)S(1)}, bf16[32,4,128]{2,1,0:T(4,128)(2,1)S(1)}, u32[]{:S(2)}, u32[]{:S(2)}) collective-permute-start(bf16[32,4,128]{2,1,0:T(4,128)(2,1)S(1)} %get-tuple-element.121), channel_id=1, source_target_pairs={{0,16},{16,32},{32,48},{48,64},{64,80},{80,96},{96,112},{1,17},{17... | collective-permute-start | bytes 98312 | tf_op jit(solution)/shard_map/while/body/eval_jaxpr/ppermute | solution.py:19
  326.2 27.0 %copy-start.1 = (bf16[32,64,128]{2,1,0:T(8,128)(2,1)S(1)}, bf16[32,64,128]{2,1,0:T(8,128)(2,1)}, u32[]{:S(2)}) copy-start(bf16[32,64,128]{2,1,0:T(8,128)(2,1)} %fusion.104) | copy-start | bytes 1572868 | tf_op jit(solution)/shard_map/while
  326.7 25.1 %collective-permute-start.6 = (bf16[32,72,4]{1,0,2:T(8,128)(2,1)S(1)}, bf16[32,72,4]{1,0,2:T(8,128)(2,1)S(1)}, u32[]{:S(2)}, u32[]{:S(2)}) collective-permute-start(bf16[32,72,4]{1,0,2:T(8,128)(2,1)S(1)} %copy.48), channel_id=1, source_target_pairs={{1,0},{2,1},{3,2},{4,3},{5,4},{6,5},{7,6},{8,7},{9,8},{10,9},{11,1... | collective-permute-start | bytes 55304 | tf_op jit(solution)/shard_map/while/body/eval_jaxpr/ppermute | solution.py:21
  328.4 24.4 %collective-permute-start.7 = (bf16[32,72,4]{1,0,2:T(8,128)(2,1)S(1)}, bf16[32,72,4]{1,0,2:T(8,128)(2,1)S(1)}, u32[]{:S(2)}, u32[]{:S(2)}) collective-permute-start(bf16[32,72,4]{1,0,2:T(8,128)(2,1)S(1)} %copy.50), channel_id=1, source_target_pairs={{0,1},{1,2},{2,3},{3,4},{4,5},{5,6},{6,7},{7,8},{8,9},{9,10},{10,1... | collective-permute-start | bytes 55304 | tf_op jit(solution)/shard_map/while/body/eval_jaxpr/ppermute | solution.py:19
Sparse Core Ops, SparseCore 0:
  369.4 130.1 reduce-scatter.3
where the time goes:
time: 513 us; the launch traced here: 511 us
  starting transfers between devices  224 us (44%)
  waiting for transfers between devices  171 us (33%)
  local copies, waits for them, and re-layouts  54.7 us (11%)
  matrix products  37.5 us (7%)
  between operations  13.4 us (3%)
  other arithmetic  9.06 us (2%)
    ppermute x20, starting transfers between devices, padded_2(): lax.ppermute(tail, axis, [(i, (i + 1) % count) for i in range(ends)])  185 us
    unnamed x2, waiting for transfers between devices  130 us
    ppermute x20, starting transfers between devices, padded_2(): lax.ppermute(head, axis, [((i + 1) % count, i) for i in range(ends)])  39 us
    ppermute x20, waiting for transfers between devices, padded_2(): lax.ppermute(tail, axis, [(i, (i + 1) % count) for i in range(ends)])  22.7 us
    dot_general x5, matrix products, cut_window(): jnp.einsum('fin,fjn->fij', picked_rows, col_table, preferred_element_type...  19.4 us
    ppermute x20, waiting for transfers between devices, padded_2(): lax.ppermute(head, axis, [((i + 1) % count, i) for i in range(ends)])  17.7 us
    unnamed x7, local copies, waits for them, and re-layouts  14.4 us
    slice x25, local copies, waits for them, and re-layouts, padded_2(): lax.slice_in_dim(cells, cells.shape[dim] - width, cells.shape[dim], axis=...  11.3 us
  transfers between devices with their start and end apart: 41, of which 30 were waited for; matrix products, arithmetic and copies ran while one was open for 1% of the time, Pallas kernels for 0%

commit v1 on v0

v1 whole, which is shorter than its diff:
```python
import jax
import jax.numpy as jnp
from jax import lax
from jax.experimental import pallas as pl
from jax.experimental.pallas import tpu as pltpu
from jax.sharding import PartitionSpec as P

SHIFT_MAX = 32
RADIUS = 4
CHUNKS = 2
HALO = SHIFT_MAX + RADIUS
SIDE = 40
PACK = 3


def rows_kernel(shift_ref, edge_ref, raw_ref, up_ref, down_ref, reg_ref, left_ref, right_ref, pad_ref):
    frames, rows, lanes = raw_ref.shape
    tall = rows + 2 * RADIUS
    index = lax.broadcasted_iota(jnp.int32, (tall, lanes), 0)
    lane = lax.broadcasted_iota(jnp.int32, (tall, lanes), 1)
    keep = (index >= edge_ref[0]) & (index < edge_ref[1])

    def group(g, count):
        lefts, rights = [], []
        for j in range(count):
            t = g * PACK + j
            pad_ref[j, 0:SIDE] = up_ref[t].astype(jnp.float32)
            pad_ref[j, SIDE : SIDE + rows] = raw_ref[t].astype(jnp.float32)
            pad_ref[j, SIDE + rows :] = down_ref[t].astype(jnp.float32)
            start = SIDE - RADIUS - shift_ref[t, 0]
            picked = jnp.where(keep, pad_ref[j, pl.ds(start, tall), :], 0.0)
            reg_ref[t] = picked.astype(jnp.bfloat16)
            lefts.append(picked if j == 0 else pltpu.roll(picked, HALO * j, 1))
            rights.append(pltpu.roll(picked, HALO * (j + 1), 1))
        left, right = lefts[0], rights[0]
        for j in range(1, count):
            left = jnp.where(lane < HALO * j, left, lefts[j])
            right = jnp.where(lane < HALO * j, right, rights[j])
        left_ref[g] = left.astype(jnp.bfloat16)
        right_ref[g] = right.astype(jnp.bfloat16)

    whole = frames // PACK
    lax.fori_loop(0, whole, lambda g, c: (group(g, PACK), c)[1], 0)
    if frames % PACK:
        group(whole, frames % PACK)


def columns_kernel(shift_ref, reg_ref, west_ref, east_ref, row_band_ref, col_band_ref, out_ref):
    frames, tall, lanes = reg_ref.shape
    rows = tall - 2 * RADIUS
    lane = lax.broadcasted_iota(jnp.int32, (tall, lanes), 1)

    def group(g, count):
        west = west_ref[g].astype(jnp.float32)
        east = east_ref[g].astype(jnp.float32)
        for j in range(count):
            t = g * PACK + j
            shift = shift_ref[t, 1]
            spot = (lanes - HALO * j) % lanes
            from_east = east if spot == 0 else pltpu.roll(east, spot, 1)
            from_west = pltpu.roll(west, (lanes - HALO - HALO * j) % lanes, 1)
            around = jnp.where(lane < lanes // 2, from_east, from_west)
            turn = (shift + lanes) & (lanes - 1)
            own = pltpu.roll(reg_ref[t].astype(jnp.float32), turn, 1)
            around = pltpu.roll(around, turn, 1)
            inside = (lane >= shift) & (lane < shift + lanes)
            mid = jnp.where(inside, own, around)
            rest = jnp.where(inside, around, own)
            window = jnp.concatenate([mid, rest], axis=1).astype(jnp.bfloat16)
            low = jnp.dot(row_band_ref[...], window, preferred_element_type=jnp.float32)
            low = jnp.dot(
                low.astype(jnp.bfloat16), col_band_ref[...], preferred_element_type=jnp.float32
            )
            out_ref[t] = (mid[RADIUS : RADIUS + rows] - low).astype(jnp.bfloat16)

    whole = frames // PACK
    lax.fori_loop(0, whole, lambda g, c: (group(g, PACK), c)[1], 0)
    if frames % PACK:
        group(whole, frames % PACK)


def tap():
    return jnp.float32(1.0 / (2 * RADIUS + 1))


def row_band(rows):
    shape = (rows, rows + 2 * RADIUS)
    offset = lax.broadcasted_iota(jnp.int32, shape, 1) - lax.broadcasted_iota(jnp.int32, shape, 0)
    return jnp.where((offset >= 0) & (offset <= 2 * RADIUS), tap(), 0.0).astype(jnp.bfloat16)


def col_band(cols, first, width):
    shape = (2 * cols, cols)
    spot = lax.broadcasted_iota(jnp.int32, shape, 0)
    col = jnp.where(spot >= cols + cols // 2, spot - 2 * cols, spot)
    near = jnp.abs(col - lax.broadcasted_iota(jnp.int32, shape, 1)) <= RADIUS
    there = (col + first >= 0) & (col + first < width)
    return jnp.where(near & there, tap(), 0.0).astype(jnp.bfloat16)


def moved(cells, axis, step):
    count = lax.axis_size(axis)
    pairs = [(i, i + step) for i in range(count) if 0 <= i + step < count]
    return lax.ppermute(cells, axis, pairs)


VMEM = pl.BlockSpec(memory_space=pltpu.VMEM)
SMEM = pl.BlockSpec(memory_space=pltpu.SMEM)
PARAMS = pltpu.CompilerParams(vmem_limit_bytes=40 * 1024 * 1024)


def body(recording, shifts, components):
    frames, rows, cols = recording.shape
    tall = rows + 2 * RADIUS
    part = frames // CHUNKS
    packs = -(-part // PACK)
    py, px = lax.axis_index("py"), lax.axis_index("px")
    height = rows * lax.axis_size("py")
    edge = jnp.stack([RADIUS - py * rows, RADIUS - py * rows + height]).astype(jnp.int32)
    bands = row_band(rows), col_band(cols, px * cols, cols * lax.axis_size("px"))
    filtered = []
    for c in range(CHUNKS):
        raw = recording[c * part : (c + 1) * part]
        shift = shifts[c * part : (c + 1) * part]
        up = moved(raw[:, rows - SIDE :], "py", 1)
        down = moved(raw[:, :SIDE], "py", -1)
        tile = jax.ShapeDtypeStruct((packs, tall, cols), jnp.bfloat16)
        reg, to_left, to_right = pl.pallas_call(
            rows_kernel,
            out_shape=(jax.ShapeDtypeStruct((part, tall, cols), jnp.bfloat16), tile, tile),
            in_specs=[SMEM, SMEM, VMEM, VMEM, VMEM],
            out_specs=(VMEM, VMEM, VMEM),
            scratch_shapes=[pltpu.VMEM((PACK, rows + 2 * SIDE, cols), jnp.float32)],
            compiler_params=PARAMS,
            cost_estimate=pl.CostEstimate(flops=10**9, bytes_accessed=10**7, transcendentals=0),
            name="rows",
        )(shift, edge, raw, up, down)
        east = moved(to_left, "px", -1)
        west = moved(to_right, "px", 1)
        filtered.append(
            pl.pallas_call(
                columns_kernel,
                out_shape=jax.ShapeDtypeStruct((part, rows, cols), jnp.bfloat16),
                in_specs=[SMEM, VMEM, VMEM, VMEM, VMEM, VMEM],
                out_specs=VMEM,
                compiler_params=PARAMS,
                cost_estimate=pl.CostEstimate(flops=10**9, bytes_accessed=10**7, transcendentals=0),
                name="columns",
            )(shift, reg, west, east, *bands)
        )
    filtered = jnp.concatenate(filtered, axis=0)
    partial = jnp.einsum(
        "fk,fij->kij", components, filtered, preferred_element_type=jnp.float32
    ).astype(jnp.bfloat16)
    return lax.psum_scatter(partial, "fr", scatter_dimension=0, tiled=True)


def solution(mesh):
    placed = (P("fr", "py", "px"), P("fr", None), P("fr", None))
    return jax.shard_map(
        body, mesh=mesh, in_specs=placed, out_specs=P("fr", "py", "px"), check_vma=False
    )
```

time: 513 us -> 259 us (0.50)
  starting transfers between devices: 224 us -> 24 us
  local copies, waits for them, and re-layouts: 54.7 us -> 13 us
  Pallas kernels: 0 us -> 34.9 us
  matrix products: 37.5 us -> 5.72 us
  other arithmetic: 9.06 us -> 0.48 us
    ppermute x40 -> x8, starting transfers between devices: 224 us -> 24 us  [moved(): return lax.ppermute(cells, axis, pairs)]
    reduce_scatter x0 -> x1, waiting for transfers between devices: none -> 164 us  [body(): return lax.psum_scatter(partial, 'fr', scatter_dimension=0, tiled=True)]
    unnamed x2 -> x1, waiting for transfers between devices: 130 us -> 0.02 us
    ppermute x40 -> x8, waiting for transfers between devices: 40.4 us -> 2.91 us  [moved(): return lax.ppermute(cells, axis, pairs)]
    pallas_call x0 -> x4, Pallas kernels: none -> 34.9 us  [the longest x2 26.4 us: body(): pl.pallas_call(columns_kernel, out_shape=jax.ShapeDtypeStruct((part, rows...]
    dot_general x11 -> x1, matrix products: 37.5 us -> 5.72 us  [body(): jnp.einsum('fk,fij->kij', components, filtered, preferred_element_type=jn...]
    unnamed x7 -> x6, local copies, waits for them, and re-layouts: 14.4 us -> 0.21 us
    ppermute x20 -> x0, local copies, waits for them, and re-layouts: 13.1 us -> none  [the longest x10 8.92 us: padded_2(): lax.ppermute(tail, axis, [(i, (i + 1) % count) for i in range(ends)])]
  transfers between devices with their start and end apart: 41 -> 9, of which waited for: 30 -> 4; matrix products, arithmetic and copies ran while one was open for 1% -> 1% of each run, Pallas kernels for 0% -> 8%
where the time goes in v1:
time: 259 us
  waiting for transfers between devices  167 us (64%)
  Pallas kernels  34.9 us (13%)
  starting transfers between devices  24 us (9%)
  between operations  13.6 us (5%)
  local copies, waits for them, and re-layouts  13 us (5%)
  matrix products  5.72 us (2%)
    reduce_scatter x1, waiting for transfers between devices, body(): return lax.psum_scatter(partial, 'fr', scatter_dimension=0, tiled=True)  164 us
    pallas_call x2, Pallas kernels, body(): pl.pallas_call(columns_kernel, out_shape=jax.ShapeDtypeStruct((part, rows...  26.4 us
    ppermute x8, starting transfers between devices, moved(): return lax.ppermute(cells, axis, pairs)  24 us
    pallas_call x2, Pallas kernels, body(): pl.pallas_call(rows_kernel, out_shape=(jax.ShapeDtypeStruct((part, tall,...  8.48 us
    convert_element_type x1, local copies, waits for them, and re-layouts, body(): partial = jnp.einsum('fk,fij->kij', components, filtered, preferred_eleme...  6.56 us
    dot_general x1, matrix products, body(): jnp.einsum('fk,fij->kij', components, filtered, preferred_element_type=jn...  5.72 us
  transfers between devices with their start and end apart: 9, of which 4 were waited for; matrix products, arithmetic and copies ran while one was open for 1% of the time, Pallas kernels for 8%

profile of v1, /device:TPU:1, one launch (start us, length us, event | category | flops | bytes accessed | tf_op | source)
XLA Modules:
  0.0 258.5 jit_solution(10203074163376918832)
XLA Ops:
  6.5 0.0 copy-start
  6.5 0.0 copy-start.1
  6.5 0.0 reduce-scatter.2.cloned.1.call-start
  6.5 3.9 %fusion.10 = (bf16[80,40,128]{2,1,0:T(8,128)(2,1)}, bf16[80,40,128]{2,1,0:T(8,128)(2,1)}, bf16[80,40,128]{2,1,0:T(8,128)(2,1)}, bf16[80,40,128]{2,1,0:T(8,128)(2,1)}) fusion(bf16[160,64,128]{2,1,0:T(8,128)(2,1)} %param.3), kind=kLoop, calls=%fused_computation.20 | loop fusion | bytes 6553600 | tf_op jit(solution)/shard_map/slice | solution.py:126
  10.4 4.5 %collective-permute-start = (bf16[80,40,128]{2,1,0:T(8,128)(2,1)}, bf16[80,40,128]{2,1,0:T(8,128)(2,1)S(1)}, u32[]{:S(2)}, u32[]{:S(2)}) collective-permute-start(bf16[80,40,128]{2,1,0:T(8,128)(2,1)} %get-tuple-element.18), channel_id=1, source_target_pairs={{0,16},{16,32},{32,48},{48,64},{64,80},{80,96},{96,112},{1,17},{17... | collective-permute-start | bytes 2457608 | tf_op jit(solution)/shard_map/ppermute | solution.py:104
  14.9 5.6 %collective-permute-start.1 = (bf16[80,40,128]{2,1,0:T(8,128)(2,1)}, bf16[80,40,128]{2,1,0:T(8,128)(2,1)S(1)}, u32[]{:S(2)}, u32[]{:S(2)}) collective-permute-start(bf16[80,40,128]{2,1,0:T(8,128)(2,1)} %get-tuple-element.17), channel_id=1, source_target_pairs={{16,0},{32,16},{48,32},{64,48},{80,64},{96,80},{112,96},{17,1},{33... | collective-permute-start | bytes 2457608 | tf_op jit(solution)/shard_map/ppermute | solution.py:104
  20.5 1.9 collective-permute-start.4
  22.4 2.5 collective-permute-start.5
  24.9 0.0 copy-done.1
  24.9 0.1 fusion.12
  25.0 0.1 copy.12.shift_ref
  25.1 0.1 copy.13.shift_ref
  25.2 0.1 pad_add_fusion.edge_ref
  25.3 2.3 fusion.11
  27.5 0.0 collective-permute-done.up_ref
  27.6 1.2 collective-permute-done.1.down_ref
  28.8 4.2 %rows.2 = (bf16[80,72,128]{2,1,0:T(8,128)(2,1)S(1)}, bf16[27,72,128]{2,1,0:T(8,128)(2,1)S(1)}, bf16[27,72,128]{2,1,0:T(8,128)(2,1)S(1)}) custom-call(s32[80,2]{1,0:T(8,128)S(1)} %copy.12.shift_ref, s32[2]{0:T(128)S(1)} %pad_add_fusion.edge_ref, bf16[80,64,128]{2,1,0:T(8,128)(2,1)S(1)} %get-tuple-element.21.raw_ref, ...), custom_call_target="tpu_custom_call" | custom-call | flops 1000000000 | bytes 10000000 | tf_op jit(solution)/shard_map/rows/pallas_call | solution.py:128
  33.0 3.2 %collective-permute-start.2 = (bf16[27,72,128]{2,1,0:T(8,128)(2,1)S(1)}, bf16[27,72,128]{2,1,0:T(8,128)(2,1)S(1)}, u32[]{:S(2)}, u32[]{:S(2)}) collective-permute-start(bf16[27,72,128]{2,1,0:T(8,128)(2,1)S(1)} %get-tuple-element.12), channel_id=1, source_target_pairs={{0,1},{1,2},{2,3},{3,4},{4,5},{5,6},{6,7},{7,8},{8,9},{9,10},{10,1... | collective-permute-start | bytes 1493000 | tf_op jit(solution)/shard_map/ppermute | solution.py:104
  36.3 1.3 collective-permute-start.3
  37.6 0.0 collective-permute-done.4.up_ref
  37.6 0.3 collective-permute-done.5.down_ref
  37.9 4.2 %rows.3 = (bf16[80,72,128]{2,1,0:T(8,128)(2,1)S(1)}, bf16[27,72,128]{2,1,0:T(8,128)(2,1)S(1)}, bf16[27,72,128]{2,1,0:T(8,128)(2,1)S(1)}) custom-call(s32[80,2]{1,0:T(8,128)S(1)} %copy.13.shift_ref, s32[2]{0:T(128)S(1)} %pad_add_fusion.edge_ref, bf16[80,64,128]{2,1,0:T(8,128)(2,1)S(1)} %get-tuple-element.22.raw_ref, ...), custom_call_target="tpu_custom_call" | custom-call | flops 1000000000 | bytes 10000000 | tf_op jit(solution)/shard_map/rows/pallas_call | solution.py:128
  42.1 3.8 %collective-permute-start.6 = (bf16[27,72,128]{2,1,0:T(8,128)(2,1)S(1)}, bf16[27,72,128]{2,1,0:T(8,128)(2,1)S(1)}, u32[]{:S(2)}, u32[]{:S(2)}) collective-permute-start(bf16[27,72,128]{2,1,0:T(8,128)(2,1)S(1)} %get-tuple-element.15), channel_id=1, source_target_pairs={{0,1},{1,2},{2,3},{3,4},{4,5},{5,6},{6,7},{7,8},{8,9},{9,10},{10,1... | collective-permute-start | bytes 1493000 | tf_op jit(solution)/shard_map/ppermute | solution.py:104
  45.9 1.3 collective-permute-start.7
  47.2 0.1 select_convert_fusion.col_band_ref
  47.4 0.0 collective-permute-done.2.west_ref
  47.4 1.4 collective-permute-done.3.east_ref
  48.8 13.2 %columns.2 = bf16[80,64,128]{2,1,0:T(8,128)(2,1)S(1)} custom-call(s32[80,2]{1,0:T(8,128)S(1)} %copy.12.shift_ref, bf16[80,72,128]{2,1,0:T(8,128)(2,1)S(1)} %get-tuple-element.11.reg_ref, bf16[27,72,128]{2,1,0:T(8,128)(2,1)S(1)} %collective-permute-done.2.west_ref, bf16[27,72,128]{2,1,0:T(8,128)(2,1)S(1)} %collective-permute-done.3.east_ref, ...), custom_call_target="tpu_custom_call" | custom-call | flops 1000000000 | bytes 10000000 | tf_op jit(solution)/shard_map/columns/pallas_call | solution.py:141
  62.0 0.0 collective-permute-done.6.west_ref
  62.0 0.0 collective-permute-done.7.east_ref
  62.0 13.2 %columns.3 = bf16[80,64,128]{2,1,0:T(8,128)(2,1)S(1)} custom-call(s32[80,2]{1,0:T(8,128)S(1)} %copy.13.shift_ref, bf16[80,72,128]{2,1,0:T(8,128)(2,1)S(1)} %get-tuple-element.14.reg_ref, bf16[27,72,128]{2,1,0:T(8,128)(2,1)S(1)} %collective-permute-done.6.west_ref, bf16[27,72,128]{2,1,0:T(8,128)(2,1)S(1)} %collective-permute-done.7.east_ref, ...), custom_call_target="tpu_custom_call" | custom-call | flops 1000000000 | bytes 10000000 | tf_op jit(solution)/shard_map/columns/pallas_call | solution.py:141
  75.2 0.2 pad_maximum_fusion
  75.5 0.0 copy-done
  75.5 5.7 %convert_bitcast_fusion = bf16[256,64,128]{0,2,1:T(8,128)(2,1)} fusion(bf16[160,64,128]{2,1,0:T(8,128)(2,1)S(1)} %pad_maximum_fusion, bf16[160,256]{1,0:T(8,128)(2,1)S(1)} %copy-done), kind=kOutput, calls=%fused_computation | convolution fusion | flops 673185792 | bytes 6897664 | tf_op jit(solution)/shard_map/fk,fij->kij/dot_general | solution.py:152
  81.2 6.6 %copy.11 = bf16[256,64,128]{2,1,0:T(8,128)(2,1)} copy(bf16[256,64,128]{0,2,1:T(8,128)(2,1)} %convert_bitcast_fusion) | data formatting | bytes 8388608 | tf_op jit(solution)/shard_map/convert_element_type | solution.py:154
  87.8 0.0 reduce-scatter.2.cloned.1.call-update
  87.8 163.9 %reduce-scatter.2.cloned.1.call-done = bf16[64,64,128]{2,1,0:T(8,128)(2,1)} async-done(((bf16[256,64,128]{2,1,0:T(8,128)(2,1)}), bf16[64,64,128]{2,1,0:T(8,128)(2,1)}) %reduce-scatter.2.cloned.1.call-update) | async-done | bytes 1048592 | tf_op jit(solution)/shard_map/reduce_scatter | solution.py:155
  (3 shorter events, 0.0 us)
Async XLA Ops:
  6.5 69.0 %copy-start = (bf16[160,256]{1,0:T(8,128)(2,1)S(1)}, bf16[160,256]{1,0:T(8,128)(2,1)}, u32[]{:S(2)}) copy-start(bf16[160,256]{1,0:T(8,128)(2,1)} %param.5) | copy-start | bytes 245764
  6.5 18.4 %copy-start.1 = (s32[160,2]{0,1:T(2,128)S(1)}, s32[160,2]{0,1:T(2,128)}, u32[]{:S(2)}) copy-start(s32[160,2]{0,1:T(2,128)} %param.4) | copy-start | bytes 3844
  6.5 245.1 %reduce-scatter.2.cloned.1.call-start = ((), (), s32[]{:S(2)}) async-start(), calls=%async_computation.1 | async-start | bytes 5242880 | tf_op jit(solution)/shard_map/reduce_scatter | solution.py:155
  10.4 17.1 %collective-permute-start = (bf16[80,40,128]{2,1,0:T(8,128)(2,1)}, bf16[80,40,128]{2,1,0:T(8,128)(2,1)S(1)}, u32[]{:S(2)}, u32[]{:S(2)}) collective-permute-start(bf16[80,40,128]{2,1,0:T(8,128)(2,1)} %get-tuple-element.18), channel_id=1, source_target_pairs={{0,16},{16,32},{32,48},{48,64},{64,80},{80,96},{96,112},{1,17},{17... | collective-permute-start | bytes 2457608 | tf_op jit(solution)/shard_map/ppermute | solution.py:104
  14.9 13.9 %collective-permute-start.1 = (bf16[80,40,128]{2,1,0:T(8,128)(2,1)}, bf16[80,40,128]{2,1,0:T(8,128)(2,1)S(1)}, u32[]{:S(2)}, u32[]{:S(2)}) collective-permute-start(bf16[80,40,128]{2,1,0:T(8,128)(2,1)} %get-tuple-element.17), channel_id=1, source_target_pairs={{16,0},{32,16},{48,32},{64,48},{80,64},{96,80},{112,96},{17,1},{33... | collective-permute-start | bytes 2457608 | tf_op jit(solution)/shard_map/ppermute | solution.py:104
  20.5 17.1 %collective-permute-start.4 = (bf16[80,40,128]{2,1,0:T(8,128)(2,1)}, bf16[80,40,128]{2,1,0:T(8,128)(2,1)S(1)}, u32[]{:S(2)}, u32[]{:S(2)}) collective-permute-start(bf16[80,40,128]{2,1,0:T(8,128)(2,1)} %get-tuple-element.20), channel_id=1, source_target_pairs={{0,16},{16,32},{32,48},{48,64},{64,80},{80,96},{96,112},{1,17},{17... | collective-permute-start | bytes 2457608 | tf_op jit(solution)/shard_map/ppermute | solution.py:104
  22.4 15.4 %collective-permute-start.5 = (bf16[80,40,128]{2,1,0:T(8,128)(2,1)}, bf16[80,40,128]{2,1,0:T(8,128)(2,1)S(1)}, u32[]{:S(2)}, u32[]{:S(2)}) collective-permute-start(bf16[80,40,128]{2,1,0:T(8,128)(2,1)} %get-tuple-element.19), channel_id=1, source_target_pairs={{16,0},{32,16},{48,32},{64,48},{80,64},{96,80},{112,96},{17,1},{33... | collective-permute-start | bytes 2457608 | tf_op jit(solution)/shard_map/ppermute | solution.py:104
  33.0 14.3 %collective-permute-start.2 = (bf16[27,72,128]{2,1,0:T(8,128)(2,1)S(1)}, bf16[27,72,128]{2,1,0:T(8,128)(2,1)S(1)}, u32[]{:S(2)}, u32[]{:S(2)}) collective-permute-start(bf16[27,72,128]{2,1,0:T(8,128)(2,1)S(1)} %get-tuple-element.12), channel_id=1, source_target_pairs={{0,1},{1,2},{2,3},{3,4},{4,5},{5,6},{6,7},{7,8},{8,9},{9,10},{10,1... | collective-permute-start | bytes 1493000 | tf_op jit(solution)/shard_map/ppermute | solution.py:104
  36.3 12.5 %collective-permute-start.3 = (bf16[27,72,128]{2,1,0:T(8,128)(2,1)S(1)}, bf16[27,72,128]{2,1,0:T(8,128)(2,1)S(1)}, u32[]{:S(2)}, u32[]{:S(2)}) collective-permute-start(bf16[27,72,128]{2,1,0:T(8,128)(2,1)S(1)} %get-tuple-element.13), channel_id=1, source_target_pairs={{1,0},{2,1},{3,2},{4,3},{5,4},{6,5},{7,6},{8,7},{9,8},{10,9},{11,1... | collective-permute-start | bytes 1493000 | tf_op jit(solution)/shard_map/ppermute | solution.py:104
  42.1 19.9 %collective-permute-start.6 = (bf16[27,72,128]{2,1,0:T(8,128)(2,1)S(1)}, bf16[27,72,128]{2,1,0:T(8,128)(2,1)S(1)}, u32[]{:S(2)}, u32[]{:S(2)}) collective-permute-start(bf16[27,72,128]{2,1,0:T(8,128)(2,1)S(1)} %get-tuple-element.15), channel_id=1, source_target_pairs={{0,1},{1,2},{2,3},{3,4},{4,5},{5,6},{6,7},{7,8},{8,9},{9,10},{10,1... | collective-permute-start | bytes 1493000 | tf_op jit(solution)/shard_map/ppermute | solution.py:104
  45.9 16.1 %collective-permute-start.7 = (bf16[27,72,128]{2,1,0:T(8,128)(2,1)S(1)}, bf16[27,72,128]{2,1,0:T(8,128)(2,1)S(1)}, u32[]{:S(2)}, u32[]{:S(2)}) collective-permute-start(bf16[27,72,128]{2,1,0:T(8,128)(2,1)S(1)} %get-tuple-element.16), channel_id=1, source_target_pairs={{1,0},{2,1},{3,2},{4,3},{5,4},{6,5},{7,6},{8,7},{9,8},{10,9},{11,1... | collective-permute-start | bytes 1493000 | tf_op jit(solution)/shard_map/ppermute | solution.py:104
Sparse Core Ops, SparseCore 0:
  87.9 163.6 reduce-scatter.1

commit v2 on v1

--- a/solution.py
+++ b/solution.py
@@ -1,3 +1,5 @@
+import functools
+
 import jax
 import jax.numpy as jnp
 from jax import lax
@@ -10,6 +12,8 @@
 CHUNKS = 2
 HALO = SHIFT_MAX + RADIUS
 SIDE = 40
+RING = 4
+ROW_CHUNKS = 4
 PACK = 3
 
 
@@ -45,20 +49,25 @@
         group(whole, frames % PACK)
 
 
-def columns_kernel(shift_ref, reg_ref, west_ref, east_ref, row_band_ref, col_band_ref, out_ref):
+def columns_kernel(
+    shift_ref, turned_ref, reg_ref, west_ref, west_far_ref, east_ref, east_far_ref, row_band_ref, col_band_ref, out_ref
+):
     frames, tall, lanes = reg_ref.shape
     rows = tall - 2 * RADIUS
     lane = lax.broadcasted_iota(jnp.int32, (tall, lanes), 1)
 
-    def group(g, count):
-        west = west_ref[g].astype(jnp.float32)
-        east = east_ref[g].astype(jnp.float32)
+    def group(first, count):
+        mids, lows = [], []
         for j in range(count):
-            t = g * PACK + j
+            t = first + j
+            if j % PACK == 0:
+                g = (first + j) // PACK if isinstance(first, int) else lax.div(first, PACK) + j // PACK
+                west = jnp.where(turned_ref[0] == 1, west_far_ref[g], west_ref[g]).astype(jnp.float32)
+                east = jnp.where(turned_ref[1] == 1, east_far_ref[g], east_ref[g]).astype(jnp.float32)
             shift = shift_ref[t, 1]
-            spot = (lanes - HALO * j) % lanes
+            spot = (lanes - HALO * (j % PACK)) % lanes
             from_east = east if spot == 0 else pltpu.roll(east, spot, 1)
-            from_west = pltpu.roll(west, (lanes - HALO - HALO * j) % lanes, 1)
+            from_west = pltpu.roll(west, (lanes - HALO - HALO * (j % PACK)) % lanes, 1)
             around = jnp.where(lane < lanes // 2, from_east, from_west)
             turn = (shift + lanes) & (lanes - 1)
             own = pltpu.roll(reg_ref[t].astype(jnp.float32), turn, 1)
@@ -68,15 +77,39 @@
             rest = jnp.where(inside, around, own)
             window = jnp.concatenate([mid, rest], axis=1).astype(jnp.bfloat16)
             low = jnp.dot(row_band_ref[...], window, preferred_element_type=jnp.float32)
-            low = jnp.dot(
-                low.astype(jnp.bfloat16), col_band_ref[...], preferred_element_type=jnp.float32
-            )
-            out_ref[t] = (mid[RADIUS : RADIUS + rows] - low).astype(jnp.bfloat16)
-
-    whole = frames // PACK
-    lax.fori_loop(0, whole, lambda g, c: (group(g, PACK), c)[1], 0)
-    if frames % PACK:
-        group(whole, frames % PACK)
+            mids.append(mid[RADIUS : RADIUS + rows])
+            lows.append(low.astype(jnp.bfloat16))
+        low = jnp.dot(
+            jnp.concatenate(lows, axis=0), col_band_ref[...], preferred_element_type=jnp.float32
+        )
+        where = first * rows if isinstance(first, int) else pl.multiple_of(first * rows, rows)
+        out_ref[pl.ds(where, count * rows), :] = jnp.concatenate(mids, axis=0) - low
+
+    step = 2 * PACK
+    whole = frames // step
+    lax.fori_loop(0, whole, lambda g, c: (group(g * step, step), c)[1], 0)
+    if frames % step:
+        group(whole * step, frames % step)
+
+
+def project_kernel(first, tile_rows, weight_ref, *refs):
+    *parts, keep_ref, pass_ref, send_ref = refs
+    count, comps, lanes = keep_ref.shape
+
+    def one(i, carry):
+        columns = [
+            part[pl.ds(first + i, part.shape[0] // tile_rows, stride=tile_rows), :] for part in parts
+        ]
+        picture = jnp.concatenate(columns, axis=0).astype(jnp.bfloat16)
+        total = jnp.dot(weight_ref[...], picture, preferred_element_type=jnp.float32)
+        total = total.astype(jnp.bfloat16)
+        keep_ref[i] = total[:comps]
+        pass_ref[i] = total[comps : 2 * comps]
+        send_ref[0, i] = total[2 * comps : 3 * comps]
+        send_ref[1, i] = total[3 * comps :]
+        return carry
+
+    lax.fori_loop(0, count, one, 0)
 
 
 def tap():
@@ -102,6 +135,23 @@
     count = lax.axis_size(axis)
     pairs = [(i, i + step) for i in range(count) if 0 <= i + step < count]
     return lax.ppermute(cells, axis, pairs)
+
+
+def moved_px(cells, step, ring_first):
+    count = lax.axis_size("px")
+    ring = min(RING, count)
+    last = ring - 1 if step == 1 else 0
+    start = 0 if step == 1 else ring - 1
+    around = [(i, i - i % ring + (i + step) % ring) for i in range(count)]
+    def far(at):
+        return [(i, i + step * ring) for i in range(at, count, ring) if 0 <= i + step * ring < count]
+    if ring_first:
+        near = lax.ppermute(cells, "px", around)
+        return near, lax.ppermute(near, "px", far(start))
+    landed = lax.ppermute(cells, "px", far(last))
+    at_end = lax.axis_index("px") % ring == last
+    near = lax.ppermute(jnp.where(at_end, landed, cells), "px", around)
+    return near, near
 
 
 VMEM = pl.BlockSpec(memory_space=pltpu.VMEM)
@@ -117,6 +167,8 @@
     py, px = lax.axis_index("py"), lax.axis_index("px")
     height = rows * lax.axis_size("py")
     edge = jnp.stack([RADIUS - py * rows, RADIUS - py * rows + height]).astype(jnp.int32)
+    ring = min(RING, lax.axis_size("px"))
+    turned = jnp.stack([px % ring == 0, px % ring == ring - 1]).astype(jnp.int32)
     bands = row_band(rows), col_band(cols, px * cols, cols * lax.axis_size("px"))
     filtered = []
     for c in range(CHUNKS):
@@ -135,24 +187,47 @@
             cost_estimate=pl.CostEstimate(flops=10**9, bytes_accessed=10**7, transcendentals=0),
             name="rows",
         )(shift, edge, raw, up, down)
-        east = moved(to_left, "px", -1)
-        west = moved(to_right, "px", 1)
+        east, east_far = moved_px(to_left, -1, c % 2 == 0)
+        west, west_far = moved_px(to_right, 1, c % 2 == 0)
         filtered.append(
             pl.pallas_call(
                 columns_kernel,
-                out_shape=jax.ShapeDtypeStruct((part, rows, cols), jnp.bfloat16),
-                in_specs=[SMEM, VMEM, VMEM, VMEM, VMEM, VMEM],
+                out_shape=jax.ShapeDtypeStruct((part * rows, cols), jnp.float32),
+                in_specs=[SMEM, SMEM] + [VMEM] * 7,
                 out_specs=VMEM,
                 compiler_params=PARAMS,
                 cost_estimate=pl.CostEstimate(flops=10**9, bytes_accessed=10**7, transcendentals=0),
                 name="columns",
-            )(shift, reg, west, east, *bands)
+            )(shift, turned, reg, west, west_far, east, east_far, *bands)
         )
-    filtered = jnp.concatenate(filtered, axis=0)
-    partial = jnp.einsum(
-        "fk,fij->kij", components, filtered, preferred_element_type=jnp.float32
-    ).astype(jnp.bfloat16)
-    return lax.psum_scatter(partial, "fr", scatter_dimension=0, tiled=True)
+    groups = lax.axis_size("fr")
+    me = lax.axis_index("fr")
+    comps = components.shape[1] // groups
+    blocks = components.T.reshape(groups, comps, frames)
+    weight = jnp.concatenate(
+        [lax.dynamic_index_in_dim(blocks, me ^ k, 0, keepdims=False) for k in (0, 2, 1, 3)], axis=0
+    )
+    count = rows // ROW_CHUNKS
+    block = jax.ShapeDtypeStruct((count, comps, cols), jnp.bfloat16)
+    pair = jax.ShapeDtypeStruct((2, count, comps, cols), jnp.bfloat16)
+    wide = jnp.float32
+    done = []
+    for c in range(ROW_CHUNKS):
+        keep, onward, send = pl.pallas_call(
+            functools.partial(project_kernel, c * count, rows),
+            out_shape=(block, block, pair),
+            in_specs=[VMEM] * (1 + CHUNKS),
+            out_specs=(VMEM, VMEM, VMEM),
+            compiler_params=PARAMS,
+            cost_estimate=pl.CostEstimate(flops=10**9, bytes_accessed=10**7, transcendentals=0),
+            name="project",
+        )(weight, *filtered)
+        near = lax.ppermute(send, "fr", [(i, i ^ 1) for i in range(groups)])
+        onward = (onward.astype(wide) + near[1].astype(wide)).astype(jnp.bfloat16)
+        far = lax.ppermute(onward, "fr", [(i, i ^ 2) for i in range(groups)])
+        total = keep.astype(wide) + near[0].astype(wide) + far.astype(wide)
+        done.append(total.astype(jnp.bfloat16))
+    return jnp.concatenate(done, axis=0).transpose(1, 0, 2)
 
 
 def solution(mesh):

time: 259 us -> 227 us (0.88)
  the two profiles are of different devices: /device:TPU:1 before, /device:TPU:29 now
where the time goes in v2:
time: 227 us; the launch traced here: 226 us
  waiting for transfers between devices  81.6 us (36%)
  starting transfers between devices  77.7 us (34%)
  Pallas kernels  41.9 us (18%)
  local copies, waits for them, and re-layouts  16.6 us (7%)
  other arithmetic  7.37 us (3%)
    ppermute x4, waiting for transfers between devices, body(): near = lax.ppermute(send, 'fr', [(i, i ^ 1) for i in range(groups)])  36.3 us
    ppermute x2, starting transfers between devices, moved_px(): near = lax.ppermute(jnp.where(at_end, landed, cells), 'px', around)  29.6 us
    ppermute x2, waiting for transfers between devices, moved_px(): return (near, lax.ppermute(near, 'px', far(start)))  23.3 us
    pallas_call x2, Pallas kernels, body(): pl.pallas_call(columns_kernel, out_shape=jax.ShapeDtypeStruct((part * row...  16.6 us
    pallas_call x4, Pallas kernels, body(): pl.pallas_call(functools.partial(project_kernel, c * count, rows), out_sh...  15.8 us
    ppermute x4, waiting for transfers between devices, body(): far = lax.ppermute(onward, 'fr', [(i, i ^ 2) for i in range(groups)])  13.3 us
    ppermute x2, starting transfers between devices, moved_px(): landed = lax.ppermute(cells, 'px', far(last))  11 us
    ppermute x4, starting transfers between devices, moved(): return lax.ppermute(cells, axis, pairs)  10.9 us
  transfers between devices with their start and end apart: 20, of which 8 were waited for; matrix products, arithmetic and copies ran while one was open for 5% of the time, Pallas kernels for 13%

profile of v2, /device:TPU:29, one launch (start us, length us, event | category | flops | bytes accessed | tf_op | source)
XLA Modules:
  0.0 225.6 jit_solution(12392397632868765637)
XLA Ops:
  0.0 3.6 %fusion.20 = (bf16[80,40,128]{2,1,0:T(8,128)(2,1)S(1)}, bf16[80,40,128]{2,1,0:T(8,128)(2,1)}, bf16[80,40,128]{2,1,0:T(8,128)(2,1)}, bf16[80,40,128]{2,1,0:T(8,128)(2,1)}) fusion(bf16[160,64,128]{2,1,0:T(8,128)(2,1)} %param.3), kind=kLoop, calls=%fused_computation.53 | loop fusion | bytes 6553600 | tf_op jit(solution)/shard_map/slice | solution.py:178
  3.6 3.4 %collective-permute-start.6 = (bf16[80,40,128]{2,1,0:T(8,128)(2,1)}, bf16[80,40,128]{2,1,0:T(8,128)(2,1)S(1)}, u32[]{:S(2)}, u32[]{:S(2)}) collective-permute-start(bf16[80,40,128]{2,1,0:T(8,128)(2,1)} %get-tuple-element.44), channel_id=1, source_target_pairs={{0,16},{16,32},{32,48},{48,64},{64,80},{80,96},{96,112},{1,17},{17... | collective-permute-start | bytes 2457608 | tf_op jit(solution)/shard_map/ppermute | solution.py:137
  7.0 1.9 collective-permute-start.7
  8.9 3.6 %collective-permute-start = (bf16[80,40,128]{2,1,0:T(8,128)(2,1)}, bf16[80,40,128]{2,1,0:T(8,128)(2,1)S(1)}, u32[]{:S(2)}, u32[]{:S(2)}) collective-permute-start(bf16[80,40,128]{2,1,0:T(8,128)(2,1)} %get-tuple-element.43), channel_id=1, source_target_pairs={{0,16},{16,32},{32,48},{48,64},{64,80},{80,96},{96,112},{1,17},{17... | collective-permute-start | bytes 2457608 | tf_op jit(solution)/shard_map/ppermute | solution.py:137
  12.6 1.9 collective-permute-start.1
  14.6 0.1 copy.16.shift_ref
  14.7 0.1 pad_add_fusion.edge_ref
  14.8 3.3 %fusion.21 = (bf16[80,64,128]{2,1,0:T(8,128)(2,1)S(1)}, bf16[80,64,128]{2,1,0:T(8,128)(2,1)}) fusion(bf16[160,64,128]{2,1,0:T(8,128)(2,1)} %param.3), kind=kLoop, calls=%fused_computation.54 | loop fusion | bytes 5242880 | tf_op jit(solution)/shard_map/slice | solution.py:175
  18.1 0.9 copy-done.4
  19.0 1.9 collective-permute-done.7.down_ref
  20.9 0.9 copy-done.6
  21.8 1.1 copy-done.5
  23.0 1.1 copy-done.7
  24.1 4.2 %rows.3 = (bf16[80,72,128]{2,1,0:T(8,128)(2,1)S(1)}, bf16[27,72,128]{2,1,0:T(8,128)(2,1)S(1)}, bf16[27,72,128]{2,1,0:T(8,128)(2,1)S(1)}) custom-call(s32[80,2]{1,0:T(8,128)S(1)} %copy.16.shift_ref, s32[2]{0:T(128)S(1)} %pad_add_fusion.edge_ref, bf16[80,64,128]{2,1,0:T(8,128)(2,1)S(1)} %get-tuple-element.45.raw_ref, bf16[80,40,128]{2,1,0:T(8,128)(2,1)S(1)} %copy-done.5, ...), custom_call_target="tpu_custom_call" | custom-call | flops 1000000000 | bytes 10000000 | tf_op jit(solution)/shard_map/rows/pallas_call | solution.py:180
  28.4 1.5 collective-permute-start.10
  29.8 0.6 select_convert_fusion.1.row_band_ref
  30.4 9.6 %collective-permute-start.8 = (bf16[27,72,128]{2,1,0:T(8,128)(2,1)S(1)}, bf16[27,72,128]{2,1,0:T(8,128)(2,1)}, u32[]{:S(2)}, u32[]{:S(2)}) collective-permute-start(bf16[27,72,128]{2,1,0:T(8,128)(2,1)S(1)} %get-tuple-element.27), channel_id=1, source_target_pairs={{3,7},{7,11},{11,15},{19,23},{23,27},{27,31},{35,39},{39,43},{43,4... | collective-permute-start | bytes 1493000 | tf_op jit(solution)/shard_map/ppermute | solution.py:151
  40.0 0.6 iota_add_fusion
  40.6 0.1 copy.15.shift_ref
  40.7 1.0 copy.11
  41.7 0.7 dynamic-slice_bitcast_fusion.3
  42.4 1.3 copy-done.2
  43.7 5.2 %rows.2 = (bf16[80,72,128]{2,1,0:T(8,128)(2,1)S(1)}, bf16[27,72,128]{2,1,0:T(8,128)(2,1)}, bf16[27,72,128]{2,1,0:T(8,128)(2,1)}) custom-call(s32[80,2]{1,0:T(8,128)S(1)} %copy.15.shift_ref, s32[2]{0:T(128)S(1)} %pad_add_fusion.edge_ref, bf16[80,64,128]{2,1,0:T(8,128)(2,1)S(1)} %copy-done.2, bf16[80,40,128]{2,1,0:T(8,128)(2,1)S(1)} %collective-permute-done.up_ref, ...), custom_call_target="tpu_custom_call" | custom-call | flops 1000000000 | bytes 10000000 | tf_op jit(solution)/shard_map/rows/pallas_call | solution.py:180
  48.9 1.9 collective-permute-start.2
  50.9 3.4 %collective-permute-start.4 = (bf16[27,72,128]{2,1,0:T(8,128)(2,1)}, bf16[27,72,128]{2,1,0:T(8,128)(2,1)S(1)}, u32[]{:S(2)}, u32[]{:S(2)}) collective-permute-start(bf16[27,72,128]{2,1,0:T(8,128)(2,1)} %get-tuple-element.25), channel_id=1, source_target_pairs={{0,3},{1,0},{2,1},{3,2},{4,7},{5,4},{6,5},{7,6},{8,11},{9,8},{10,9... | collective-permute-start | bytes 1493000 | tf_op jit(solution)/shard_map/ppermute | solution.py:149
  54.2 0.9 broadcast_select_fusion
  55.2 1.9 collective-permute-start.11
  57.1 2.0 broadcast_select_fusion.1
  59.1 27.7 %collective-permute-start.9 = (bf16[27,72,128]{2,1,0:T(8,128)(2,1)}, bf16[27,72,128]{2,1,0:T(8,128)(2,1)S(1)}, u32[]{:S(2)}, u32[]{:S(2)}) collective-permute-start(bf16[27,72,128]{2,1,0:T(8,128)(2,1)} %broadcast_select_fusion.1), channel_id=1, source_target_pairs={{0,1},{1,2},{2,3},{3,0},{4,5},{5,6},{6,7},{7,4},{8,9},{9,10},{10,1... | collective-permute-start | bytes 1493000 | tf_op jit(solution)/shard_map/ppermute | solution.py:153
  86.8 0.6 iota_compare_fusion
  87.3 0.7 collective-permute-start.3
  88.0 1.3 collective-permute-start.5
  89.3 0.1 add_convert_fusion.turned_ref
  89.4 0.8 pad_maximum_fusion.weight_ref
  90.3 0.8 select_convert_fusion.col_band_ref
  91.1 4.8 %collective-permute-done.11.east_ref.east_far_ref = bf16[27,72,128]{2,1,0:T(8,128)(2,1)S(1)} collective-permute-done((bf16[27,72,128]{2,1,0:T(8,128)(2,1)}, bf16[27,72,128]{2,1,0:T(8,128)(2,1)S(1)}, u32[]{:S(2)}, u32[]{:S(2)}) %collective-permute-start.11) | collective-permute-done | bytes 497696 | tf_op jit(solution)/shard_map/ppermute | solution.py:153
  95.9 1.9 collective-permute-done.9.west_ref.west_far_ref
  97.9 0.7 copy-done.3
  98.6 8.3 %columns.3.refs_1_ = f32[5120,128]{1,0:T(8,128)S(1)} custom-call(s32[80,2]{1,0:T(8,128)S(1)} %copy.16.shift_ref, s32[2]{0:T(128)S(1)} %add_convert_fusion.turned_ref, bf16[80,72,128]{2,1,0:T(8,128)(2,1)S(1)} %get-tuple-element.26.reg_ref, bf16[27,72,128]{2,1,0:T(8,128)(2,1)S(1)} %collective-permute-done.9.west_ref.west_far_ref, ...), custom_call_target="tpu_custom_call" | custom-call | flops 1000000000 | bytes 10000000 | tf_op jit(solution)/shard_map/columns/pallas_call | solution.py:193
  106.9 23.3 %collective-permute-done.5.east_far_ref = bf16[27,72,128]{2,1,0:T(8,128)(2,1)S(1)} collective-permute-done((bf16[27,72,128]{2,1,0:T(8,128)(2,1)S(1)}, bf16[27,72,128]{2,1,0:T(8,128)(2,1)S(1)}, u32[]{:S(2)}, u32[]{:S(2)}) %collective-permute-start.5) | collective-permute-done | bytes 497696 | tf_op jit(solution)/shard_map/ppermute | solution.py:150
  130.2 8.3 %columns.2.refs_0_ = f32[5120,128]{1,0:T(8,128)S(1)} custom-call(s32[80,2]{1,0:T(8,128)S(1)} %copy.15.shift_ref, s32[2]{0:T(128)S(1)} %add_convert_fusion.turned_ref, bf16[80,72,128]{2,1,0:T(8,128)(2,1)S(1)} %copy-done.1, bf16[27,72,128]{2,1,0:T(8,128)(2,1)S(1)} %collective-permute-done.2.west_ref, ...), custom_call_target="tpu_custom_call" | custom-call | flops 1000000000 | bytes 10000000 | tf_op jit(solution)/shard_map/columns/pallas_call | solution.py:193
  138.5 4.0 %project.4 = (bf16[16,64,128]{2,1,0:T(8,128)(2,1)S(1)}, bf16[16,64,128]{2,1,0:T(8,128)(2,1)S(1)}, bf16[2,16,64,128]{3,2,1,0:T(8,128)(2,1)S(1)}) custom-call(bf16[256,160]{1,0:T(8,128)(2,1)S(1)} %pad_maximum_fusion.weight_ref, f32[5120,128]{1,0:T(8,128)S(1)} %columns.2.refs_0_, f32[5120,128]{1,0:T(8,128)S(1)} %columns.3.refs_1_), custom_call_target="tpu_custom_call" | custom-call | flops 1000000000 | bytes 10000000 | tf_op jit(solution)/shard_map/project/pallas_call | solution.py:216
  142.5 1.9 collective-permute-start.12
  144.4 4.0 %project.5 = (bf16[16,64,128]{2,1,0:T(8,128)(2,1)S(1)}, bf16[16,64,128]{2,1,0:T(8,128)(2,1)S(1)}, bf16[2,16,64,128]{3,2,1,0:T(8,128)(2,1)S(1)}) custom-call(bf16[256,160]{1,0:T(8,128)(2,1)S(1)} %pad_maximum_fusion.weight_ref, f32[5120,128]{1,0:T(8,128)S(1)} %columns.2.refs_0_, f32[5120,128]{1,0:T(8,128)S(1)} %columns.3.refs_1_), custom_call_target="tpu_custom_call" | custom-call | flops 1000000000 | bytes 10000000 | tf_op jit(solution)/shard_map/project/pallas_call | solution.py:216
  148.4 3.4 %collective-permute-start.14 = (bf16[2,16,64,128]{3,2,1,0:T(8,128)(2,1)S(1)}, bf16[2,16,64,128]{3,2,1,0:T(8,128)(2,1)S(1)}, u32[]{:S(2)}, u32[]{:S(2)}) collective-permute-start(bf16[2,16,64,128]{3,2,1,0:T(8,128)(2,1)S(1)} %get-tuple-element.33), channel_id=1, source_target_pairs={{0,128},{128,0},{256,384},{384,256},{1,129},{129,1},{257,385},{385... | collective-permute-start | bytes 1572872 | tf_op jit(solution)/shard_map/ppermute | solution.py:225
  151.7 4.0 %project.6 = (bf16[16,64,128]{2,1,0:T(8,128)(2,1)S(1)}, bf16[16,64,128]{2,1,0:T(8,128)(2,1)S(1)}, bf16[2,16,64,128]{3,2,1,0:T(8,128)(2,1)S(1)}) custom-call(bf16[256,160]{1,0:T(8,128)(2,1)S(1)} %pad_maximum_fusion.weight_ref, f32[5120,128]{1,0:T(8,128)S(1)} %columns.2.refs_0_, f32[5120,128]{1,0:T(8,128)S(1)} %columns.3.refs_1_), custom_call_target="tpu_custom_call" | custom-call | flops 1000000000 | bytes 10000000 | tf_op jit(solution)/shard_map/project/pallas_call | solution.py:216
  155.7 1.9 collective-permute-start.16
  157.6 4.0 %project.7 = (bf16[16,64,128]{2,1,0:T(8,128)(2,1)S(1)}, bf16[16,64,128]{2,1,0:T(8,128)(2,1)S(1)}, bf16[2,16,64,128]{3,2,1,0:T(8,128)(2,1)S(1)}) custom-call(bf16[256,160]{1,0:T(8,128)(2,1)S(1)} %pad_maximum_fusion.weight_ref, f32[5120,128]{1,0:T(8,128)S(1)} %columns.2.refs_0_, f32[5120,128]{1,0:T(8,128)S(1)} %columns.3.refs_1_), custom_call_target="tpu_custom_call" | custom-call | flops 1000000000 | bytes 10000000 | tf_op jit(solution)/shard_map/project/pallas_call | solution.py:216
  161.6 3.4 %collective-permute-start.18 = (bf16[2,16,64,128]{3,2,1,0:T(8,128)(2,1)S(1)}, bf16[2,16,64,128]{3,2,1,0:T(8,128)(2,1)S(1)}, u32[]{:S(2)}, u32[]{:S(2)}) collective-permute-start(bf16[2,16,64,128]{3,2,1,0:T(8,128)(2,1)S(1)} %get-tuple-element.39), channel_id=1, source_target_pairs={{0,128},{128,0},{256,384},{384,256},{1,129},{129,1},{257,385},{385... | collective-permute-start | bytes 1572872 | tf_op jit(solution)/shard_map/ppermute | solution.py:225
  165.0 0.1 fusion.9
  165.1 1.9 collective-permute-start.13
  167.0 1.6 collective-permute-done.14
  168.7 2.6 %collective-permute-start.15 = (bf16[16,64,128]{2,1,0:T(8,128)(2,1)S(1)}, bf16[16,64,128]{2,1,0:T(8,128)(2,1)S(1)}, u32[]{:S(2)}, u32[]{:S(2)}) collective-permute-start(bf16[16,64,128]{2,1,0:T(8,128)(2,1)S(1)} %fusion.6), channel_id=1, source_target_pairs={{0,256},{128,384},{256,0},{384,128},{1,257},{129,385},{257,1},{385... | collective-permute-start | bytes 786440 | tf_op jit(solution)/shard_map/ppermute | solution.py:227
  171.3 17.1 %collective-permute-done.16 = bf16[2,16,64,128]{3,2,1,0:T(8,128)(2,1)S(1)} collective-permute-done((bf16[2,16,64,128]{3,2,1,0:T(8,128)(2,1)S(1)}, bf16[2,16,64,128]{3,2,1,0:T(8,128)(2,1)S(1)}, u32[]{:S(2)}, u32[]{:S(2)}) %collective-permute-start.16) | collective-permute-done | bytes 524320 | tf_op jit(solution)/shard_map/ppermute | solution.py:225
  188.6 1.9 collective-permute-start.17
  190.5 17.5 %collective-permute-done.18 = bf16[2,16,64,128]{3,2,1,0:T(8,128)(2,1)S(1)} collective-permute-done((bf16[2,16,64,128]{3,2,1,0:T(8,128)(2,1)S(1)}, bf16[2,16,64,128]{3,2,1,0:T(8,128)(2,1)S(1)}, u32[]{:S(2)}, u32[]{:S(2)}) %collective-permute-start.18) | collective-permute-done | bytes 524320 | tf_op jit(solution)/shard_map/ppermute | solution.py:225
  208.0 1.9 collective-permute-start.19
  210.0 0.1 fusion.11
  210.1 0.1 fusion.8
  210.2 0.1 fusion.5
  210.4 13.3 %collective-permute-done.19 = bf16[16,64,128]{2,1,0:T(8,128)(2,1)S(1)} collective-permute-done((bf16[16,64,128]{2,1,0:T(8,128)(2,1)S(1)}, bf16[16,64,128]{2,1,0:T(8,128)(2,1)S(1)}, u32[]{:S(2)}, u32[]{:S(2)}) %collective-permute-start.19) | collective-permute-done | bytes 262176 | tf_op jit(solution)/shard_map/ppermute | solution.py:227
  223.7 0.1 fusion.2
  223.8 0.1 maximum_bitcast_fusion
  223.9 1.6 copy.14
  (28 shorter events, 0.3 us)
Async XLA Ops:
  0.0 14.5 %copy-start.8 = (s32[160,2]{0,1:T(2,128)S(1)}, s32[160,2]{0,1:T(2,128)}, u32[]{:S(2)}) copy-start(s32[160,2]{0,1:T(2,128)} %param.4) | copy-start | bytes 3844
  3.6 14.5 %collective-permute-start.6 = (bf16[80,40,128]{2,1,0:T(8,128)(2,1)}, bf16[80,40,128]{2,1,0:T(8,128)(2,1)S(1)}, u32[]{:S(2)}, u32[]{:S(2)}) collective-permute-start(bf16[80,40,128]{2,1,0:T(8,128)(2,1)} %get-tuple-element.44), channel_id=1, source_target_pairs={{0,16},{16,32},{32,48},{48,64},{64,80},{80,96},{96,112},{1,17},{17... | collective-permute-start | bytes 2457608 | tf_op jit(solution)/shard_map/ppermute | solution.py:137
  7.0 14.0 %collective-permute-start.7 = (bf16[80,40,128]{2,1,0:T(8,128)(2,1)S(1)}, bf16[80,40,128]{2,1,0:T(8,128)(2,1)S(1)}, u32[]{:S(2)}, u32[]{:S(2)}) collective-permute-start(bf16[80,40,128]{2,1,0:T(8,128)(2,1)S(1)} %get-tuple-element.41), channel_id=1, source_target_pairs={{16,0},{32,16},{48,32},{64,48},{80,64},{96,80},{112,96},{17,1},{33... | collective-permute-start | bytes 2457608 | tf_op jit(solution)/shard_map/ppermute | solution.py:137
  8.9 33.5 %collective-permute-start = (bf16[80,40,128]{2,1,0:T(8,128)(2,1)}, bf16[80,40,128]{2,1,0:T(8,128)(2,1)S(1)}, u32[]{:S(2)}, u32[]{:S(2)}) collective-permute-start(bf16[80,40,128]{2,1,0:T(8,128)(2,1)} %get-tuple-element.43), channel_id=1, source_target_pairs={{0,16},{16,32},{32,48},{48,64},{64,80},{80,96},{96,112},{1,17},{17... | collective-permute-start | bytes 2457608 | tf_op jit(solution)/shard_map/ppermute | solution.py:137
  12.6 29.8 %collective-permute-start.1 = (bf16[80,40,128]{2,1,0:T(8,128)(2,1)}, bf16[80,40,128]{2,1,0:T(8,128)(2,1)}, u32[]{:S(2)}, u32[]{:S(2)}) collective-permute-start(bf16[80,40,128]{2,1,0:T(8,128)(2,1)} %get-tuple-element.42), channel_id=1, source_target_pairs={{16,0},{32,16},{48,32},{64,48},{80,64},{96,80},{112,96},{17,1},{33... | collective-permute-start | bytes 2457608 | tf_op jit(solution)/shard_map/ppermute | solution.py:137
  18.1 0.9 copy-start.4
  20.9 0.9 copy-start.6
  21.8 1.1 copy-start.5
  23.0 1.1 copy-start.7
  28.4 25.8 %collective-permute-start.10 = (bf16[27,72,128]{2,1,0:T(8,128)(2,1)S(1)}, bf16[27,72,128]{2,1,0:T(8,128)(2,1)}, u32[]{:S(2)}, u32[]{:S(2)}) collective-permute-start(bf16[27,72,128]{2,1,0:T(8,128)(2,1)S(1)} %get-tuple-element.28), channel_id=1, source_target_pairs={{4,0},{8,4},{12,8},{20,16},{24,20},{28,24},{36,32},{40,36},{44,40}... | collective-permute-start | bytes 1493000 | tf_op jit(solution)/shard_map/ppermute | solution.py:151
  30.4 26.6 %collective-permute-start.8 = (bf16[27,72,128]{2,1,0:T(8,128)(2,1)S(1)}, bf16[27,72,128]{2,1,0:T(8,128)(2,1)}, u32[]{:S(2)}, u32[]{:S(2)}) collective-permute-start(bf16[27,72,128]{2,1,0:T(8,128)(2,1)S(1)} %get-tuple-element.27), channel_id=1, source_target_pairs={{3,7},{7,11},{11,15},{19,23},{23,27},{27,31},{35,39},{39,43},{43,4... | collective-permute-start | bytes 1493000 | tf_op jit(solution)/shard_map/ppermute | solution.py:151
  42.4 1.3 copy-start.2
  48.9 10.1 %copy-start = (bf16[80,72,128]{2,1,0:T(8,128)(2,1)}, bf16[80,72,128]{2,1,0:T(8,128)(2,1)S(1)}, u32[]{:S(2)}) copy-start(bf16[80,72,128]{2,1,0:T(8,128)(2,1)S(1)} %get-tuple-element.23.reg_ref) | copy-start | bytes 4423684
  48.9 38.4 %collective-permute-start.2 = (bf16[27,72,128]{2,1,0:T(8,128)(2,1)}, bf16[27,72,128]{2,1,0:T(8,128)(2,1)S(1)}, u32[]{:S(2)}, u32[]{:S(2)}) collective-permute-start(bf16[27,72,128]{2,1,0:T(8,128)(2,1)} %get-tuple-element.24), channel_id=1, source_target_pairs={{0,1},{1,2},{2,3},{3,0},{4,5},{5,6},{6,7},{7,4},{8,9},{9,10},{10,1... | collective-permute-start | bytes 1493000 | tf_op jit(solution)/shard_map/ppermute | solution.py:149
  50.9 37.2 %collective-permute-start.4 = (bf16[27,72,128]{2,1,0:T(8,128)(2,1)}, bf16[27,72,128]{2,1,0:T(8,128)(2,1)S(1)}, u32[]{:S(2)}, u32[]{:S(2)}) collective-permute-start(bf16[27,72,128]{2,1,0:T(8,128)(2,1)} %get-tuple-element.25), channel_id=1, source_target_pairs={{0,3},{1,0},{2,1},{3,2},{4,7},{5,4},{6,5},{7,6},{8,11},{9,8},{10,9... | collective-permute-start | bytes 1493000 | tf_op jit(solution)/shard_map/ppermute | solution.py:149
  55.2 40.8 %collective-permute-start.11 = (bf16[27,72,128]{2,1,0:T(8,128)(2,1)}, bf16[27,72,128]{2,1,0:T(8,128)(2,1)S(1)}, u32[]{:S(2)}, u32[]{:S(2)}) collective-permute-start(bf16[27,72,128]{2,1,0:T(8,128)(2,1)} %broadcast_select_fusion), channel_id=1, source_target_pairs={{0,3},{1,0},{2,1},{3,2},{4,7},{5,4},{6,5},{7,6},{8,11},{9,8},{10,9... | collective-permute-start | bytes 1493000 | tf_op jit(solution)/shard_map/ppermute | solution.py:153
  59.1 38.8 %collective-permute-start.9 = (bf16[27,72,128]{2,1,0:T(8,128)(2,1)}, bf16[27,72,128]{2,1,0:T(8,128)(2,1)S(1)}, u32[]{:S(2)}, u32[]{:S(2)}) collective-permute-start(bf16[27,72,128]{2,1,0:T(8,128)(2,1)} %broadcast_select_fusion.1), channel_id=1, source_target_pairs={{0,1},{1,2},{2,3},{3,0},{4,5},{5,6},{6,7},{7,4},{8,9},{9,10},{10,1... | collective-permute-start | bytes 1493000 | tf_op jit(solution)/shard_map/ppermute | solution.py:153
  87.3 19.5 %collective-permute-start.3 = (bf16[27,72,128]{2,1,0:T(8,128)(2,1)S(1)}, bf16[27,72,128]{2,1,0:T(8,128)(2,1)S(1)}, u32[]{:S(2)}, u32[]{:S(2)}) collective-permute-start(bf16[27,72,128]{2,1,0:T(8,128)(2,1)S(1)} %collective-permute-done.2.west_ref), channel_id=1, source_target_pairs={{0,4},{4,8},{8,12},{16,20},{20,24},{24,28},{32,36},{36,40},{40,44}... | collective-permute-start | bytes 1493000 | tf_op jit(solution)/shard_map/ppermute | solution.py:150
  88.0 42.1 %collective-permute-start.5 = (bf16[27,72,128]{2,1,0:T(8,128)(2,1)S(1)}, bf16[27,72,128]{2,1,0:T(8,128)(2,1)S(1)}, u32[]{:S(2)}, u32[]{:S(2)}) collective-permute-start(bf16[27,72,128]{2,1,0:T(8,128)(2,1)S(1)} %collective-permute-done.4.east_ref), channel_id=1, source_target_pairs={{7,3},{11,7},{15,11},{23,19},{27,23},{31,27},{39,35},{43,39},{47,4... | collective-permute-start | bytes 1493000 | tf_op jit(solution)/shard_map/ppermute | solution.py:150
  97.9 0.7 copy-start.3
  98.6 31.6 %copy-start.1 = (bf16[80,72,128]{2,1,0:T(8,128)(2,1)S(1)}, bf16[80,72,128]{2,1,0:T(8,128)(2,1)}, u32[]{:S(2)}) copy-start(bf16[80,72,128]{2,1,0:T(8,128)(2,1)} %copy-done) | copy-start | bytes 4423684
  142.5 22.5 %collective-permute-start.12 = (bf16[2,16,64,128]{3,2,1,0:T(8,128)(2,1)S(1)}, bf16[2,16,64,128]{3,2,1,0:T(8,128)(2,1)S(1)}, u32[]{:S(2)}, u32[]{:S(2)}) collective-permute-start(bf16[2,16,64,128]{3,2,1,0:T(8,128)(2,1)S(1)} %get-tuple-element.30), channel_id=1, source_target_pairs={{0,128},{128,0},{256,384},{384,256},{1,129},{129,1},{257,385},{385... | collective-permute-start | bytes 1572872 | tf_op jit(solution)/shard_map/ppermute | solution.py:225
  148.4 20.3 %collective-permute-start.14 = (bf16[2,16,64,128]{3,2,1,0:T(8,128)(2,1)S(1)}, bf16[2,16,64,128]{3,2,1,0:T(8,128)(2,1)S(1)}, u32[]{:S(2)}, u32[]{:S(2)}) collective-permute-start(bf16[2,16,64,128]{3,2,1,0:T(8,128)(2,1)S(1)} %get-tuple-element.33), channel_id=1, source_target_pairs={{0,128},{128,0},{256,384},{384,256},{1,129},{129,1},{257,385},{385... | collective-permute-start | bytes 1572872 | tf_op jit(solution)/shard_map/ppermute | solution.py:225
  155.7 32.8 %collective-permute-start.16 = (bf16[2,16,64,128]{3,2,1,0:T(8,128)(2,1)S(1)}, bf16[2,16,64,128]{3,2,1,0:T(8,128)(2,1)S(1)}, u32[]{:S(2)}, u32[]{:S(2)}) collective-permute-start(bf16[2,16,64,128]{3,2,1,0:T(8,128)(2,1)S(1)} %get-tuple-element.36), channel_id=1, source_target_pairs={{0,128},{128,0},{256,384},{384,256},{1,129},{129,1},{257,385},{385... | collective-permute-start | bytes 1572872 | tf_op jit(solution)/shard_map/ppermute | solution.py:225
  161.6 46.4 %collective-permute-start.18 = (bf16[2,16,64,128]{3,2,1,0:T(8,128)(2,1)S(1)}, bf16[2,16,64,128]{3,2,1,0:T(8,128)(2,1)S(1)}, u32[]{:S(2)}, u32[]{:S(2)}) collective-permute-start(bf16[2,16,64,128]{3,2,1,0:T(8,128)(2,1)S(1)} %get-tuple-element.39), channel_id=1, source_target_pairs={{0,128},{128,0},{256,384},{384,256},{1,129},{129,1},{257,385},{385... | collective-permute-start | bytes 1572872 | tf_op jit(solution)/shard_map/ppermute | solution.py:225
  165.1 44.9 %collective-permute-start.13 = (bf16[16,64,128]{2,1,0:T(8,128)(2,1)S(1)}, bf16[16,64,128]{2,1,0:T(8,128)(2,1)S(1)}, u32[]{:S(2)}, u32[]{:S(2)}) collective-permute-start(bf16[16,64,128]{2,1,0:T(8,128)(2,1)S(1)} %fusion.9), channel_id=1, source_target_pairs={{0,256},{128,384},{256,0},{384,128},{1,257},{129,385},{257,1},{385... | collective-permute-start | bytes 786440 | tf_op jit(solution)/shard_map/ppermute | solution.py:227
  168.7 41.4 %collective-permute-start.15 = (bf16[16,64,128]{2,1,0:T(8,128)(2,1)S(1)}, bf16[16,64,128]{2,1,0:T(8,128)(2,1)S(1)}, u32[]{:S(2)}, u32[]{:S(2)}) collective-permute-start(bf16[16,64,128]{2,1,0:T(8,128)(2,1)S(1)} %fusion.6), channel_id=1, source_target_pairs={{0,256},{128,384},{256,0},{384,128},{1,257},{129,385},{257,1},{385... | collective-permute-start | bytes 786440 | tf_op jit(solution)/shard_map/ppermute | solution.py:227
  188.6 21.7 %collective-permute-start.17 = (bf16[16,64,128]{2,1,0:T(8,128)(2,1)S(1)}, bf16[16,64,128]{2,1,0:T(8,128)(2,1)S(1)}, u32[]{:S(2)}, u32[]{:S(2)}) collective-permute-start(bf16[16,64,128]{2,1,0:T(8,128)(2,1)S(1)} %fusion.3), channel_id=1, source_target_pairs={{0,256},{128,384},{256,0},{384,128},{1,257},{129,385},{257,1},{385... | collective-permute-start | bytes 786440 | tf_op jit(solution)/shard_map/ppermute | solution.py:227
  208.0 15.6 %collective-permute-start.19 = (bf16[16,64,128]{2,1,0:T(8,128)(2,1)S(1)}, bf16[16,64,128]{2,1,0:T(8,128)(2,1)S(1)}, u32[]{:S(2)}, u32[]{:S(2)}) collective-permute-start(bf16[16,64,128]{2,1,0:T(8,128)(2,1)S(1)} %fusion), channel_id=1, source_target_pairs={{0,256},{128,384},{256,0},{384,128},{1,257},{129,385},{257,1},{385... | collective-permute-start | bytes 786440 | tf_op jit(solution)/shard_map/ppermute | solution.py:227

commit v3 on v2

--- a/solution.py
+++ b/solution.py
@@ -9,7 +9,7 @@
 
 SHIFT_MAX = 32
 RADIUS = 4
-CHUNKS = 2
+CHUNKS = 1
 HALO = SHIFT_MAX + RADIUS
 SIDE = 40
 RING = 4
@@ -49,9 +49,7 @@
         group(whole, frames % PACK)
 
 
-def columns_kernel(
-    shift_ref, turned_ref, reg_ref, west_ref, west_far_ref, east_ref, east_far_ref, row_band_ref, col_band_ref, out_ref
-):
+def columns_kernel(shift_ref, reg_ref, west_ref, east_ref, row_band_ref, col_band_ref, out_ref):
     frames, tall, lanes = reg_ref.shape
     rows = tall - 2 * RADIUS
     lane = lax.broadcasted_iota(jnp.int32, (tall, lanes), 1)
@@ -62,8 +60,8 @@
             t = first + j
             if j % PACK == 0:
                 g = (first + j) // PACK if isinstance(first, int) else lax.div(first, PACK) + j // PACK
-                west = jnp.where(turned_ref[0] == 1, west_far_ref[g], west_ref[g]).astype(jnp.float32)
-                east = jnp.where(turned_ref[1] == 1, east_far_ref[g], east_ref[g]).astype(jnp.float32)
+                west = west_ref[g].astype(jnp.float32)
+                east = east_ref[g].astype(jnp.float32)
             shift = shift_ref[t, 1]
             spot = (lanes - HALO * (j % PACK)) % lanes
             from_east = east if spot == 0 else pltpu.roll(east, spot, 1)
@@ -137,21 +135,188 @@
     return lax.ppermute(cells, axis, pairs)
 
 
-def moved_px(cells, step, ring_first):
+def exchange_kernel(
+    to_left, to_right, west, east, hop, second, plain_out, plain_in, out_1, in_1, out_2, in_2, out_3, in_3
+):
     count = lax.axis_size("px")
-    ring = min(RING, count)
-    last = ring - 1 if step == 1 else 0
-    start = 0 if step == 1 else ring - 1
-    around = [(i, i - i % ring + (i + step) % ring) for i in range(count)]
-    def far(at):
-        return [(i, i + step * ring) for i in range(at, count, ring) if 0 <= i + step * ring < count]
-    if ring_first:
-        near = lax.ppermute(cells, "px", around)
-        return near, lax.ppermute(near, "px", far(start))
-    landed = lax.ppermute(cells, "px", far(last))
-    at_end = lax.axis_index("px") % ring == last
-    near = lax.ppermute(jnp.where(at_end, landed, cells), "px", around)
-    return near, near
+    me = lax.axis_index("px")
+    spot, ring = lax.rem(me, RING), lax.div(me, RING)
+    rings = count // RING
+    packs = to_left.shape[0]
+    cuts = [packs * k // 6 for k in range(7)]
+    lots = [(0, 1), (2,), (3,), (4, 5)]
+
+    def piece(ref, k):
+        return ref.at[pl.ds(cuts[k], cuts[k + 1] - cuts[k])]
+
+    def kept(ref, d, i, k):
+        return ref.at[d, i, pl.ds(0, cuts[k + 1] - cuts[k])]
+
+    def copy(source, target, sent, got, px):
+        return pltpu.make_async_remote_copy(
+            src_ref=source,
+            dst_ref=target,
+            send_sem=sent,
+            recv_sem=got,
+            device_id={"px": px},
+            device_id_type=pl.DeviceIdType.MESH,
+        )
+
+    barrier = pltpu.get_barrier_semaphore()
+    for k in range(1, RING):
+        pl.semaphore_signal(
+            barrier,
+            inc=1,
+            device_id={"px": ring * RING + lax.rem(spot + k, RING)},
+            device_id_type=pl.DeviceIdType.MESH,
+        )
+    for step in (1, -1):
+        @pl.when((ring + step >= 0) & (ring + step < rings))
+        def _():
+            pl.semaphore_signal(
+                barrier,
+                inc=1,
+                device_id={"px": me + step * RING},
+                device_id_type=pl.DeviceIdType.MESH,
+            )
+    at_end = (ring == 0) | (ring == rings - 1)
+
+    @pl.when(at_end)
+    def _():
+        pl.semaphore_wait(barrier, RING)
+
+    @pl.when(jnp.logical_not(at_end))
+    def _():
+        pl.semaphore_wait(barrier, RING + 1)
+
+    sides = []
+    for d, step, source, target, first, final in (
+        (0, 1, to_right, west, RING - 1, 0),
+        (1, -1, to_left, east, 0, RING - 1),
+    ):
+        onward = (ring + step >= 0) & (ring + step < rings)
+        arriving = (ring - step >= 0) & (ring - step < rings)
+
+        def plain(d=d, step=step, source=source, target=target):
+            return copy(source, target, plain_out.at[d], plain_in.at[d], me + step)
+
+        def spread(c, i, k, d=d, source=source):
+            return copy(
+                piece(source, k), kept(hop, d, i, k), out_1.at[d, c, i], in_1.at[d, i], ring * RING + c
+            )
+
+        def cross(c, i, k, d=d, step=step, source=source, target=target, first=first, final=final):
+            return copy(
+                piece(source, k) if c == first else kept(hop, d, i, k),
+                piece(target, k) if c == final else kept(second, d, i, k),
+                out_2.at[d, i],
+                in_2.at[d, i],
+                me + step * RING,
+            )
+
+        def gather(c, i, k, d=d, target=target, final=final):
+            return copy(
+                kept(second, d, i, k),
+                piece(target, k),
+                out_3.at[d, i],
+                in_3.at[d, c, i],
+                ring * RING + final,
+            )
+
+        sides.append((target, first, final, onward, arriving, plain, spread, cross, gather))
+
+    def each(c):
+        return list(enumerate(lots[c]))
+
+    for target, first, final, onward, arriving, plain, spread, cross, gather in sides:
+        @pl.when((spot == first) & onward)
+        def _():
+            for i, k in each(first):
+                cross(first, i, k).start()
+            for c in range(RING):
+                if c != first:
+                    for i, k in each(c):
+                        spread(c, i, k).start()
+
+        @pl.when(spot != first)
+        def _():
+            plain().start()
+
+    for c in range(RING):
+        for target, first, final, onward, arriving, plain, spread, cross, gather in sides:
+            if c != first:
+                @pl.when((spot == c) & onward)
+                def _():
+                    for i, k in each(c):
+                        spread(c, i, k).wait_recv()
+                        cross(c, i, k).start()
+
+    for c in range(RING):
+        for target, first, final, onward, arriving, plain, spread, cross, gather in sides:
+            if c != final:
+                @pl.when((spot == c) & arriving)
+                def _():
+                    for i, k in each(c):
+                        cross(c, i, k).wait_recv()
+                        gather(c, i, k).start()
+
+    for target, first, final, onward, arriving, plain, spread, cross, gather in sides:
+        @pl.when((spot == final) & arriving)
+        def _():
+            for c in range(RING):
+                for i, k in each(c):
+                    (cross if c == final else gather)(c, i, k).wait_recv()
+
+        @pl.when((spot == final) & jnp.logical_not(arriving))
+        def _():
+            target[...] = jnp.zeros_like(target)
+
+        @pl.when(spot != final)
+        def _():
+            plain().wait_recv()
+
+    for target, first, final, onward, arriving, plain, spread, cross, gather in sides:
+        @pl.when((spot == first) & onward)
+        def _():
+            for c in range(RING):
+                if c != first:
+                    for i, k in each(c):
+                        spread(c, i, k).wait_send()
+
+        @pl.when(spot != first)
+        def _():
+            plain().wait_send()
+
+        for c in range(RING):
+            @pl.when((spot == c) & onward)
+            def _():
+                for i, k in each(c):
+                    cross(c, i, k).wait_send()
+
+            if c != final:
+                @pl.when((spot == c) & arriving)
+                def _():
+                    for i, k in each(c):
+                        gather(c, i, k).wait_send()
+
+
+def exchanged(to_left, to_right):
+    tile = jax.ShapeDtypeStruct(to_left.shape, to_left.dtype)
+    packs = to_left.shape[0]
+    kept = pltpu.VMEM((2, 2, -(-packs // 6)) + to_left.shape[1:], to_left.dtype)
+    sem = pltpu.SemaphoreType.DMA
+    return pl.pallas_call(
+        exchange_kernel,
+        out_shape=(tile, tile),
+        in_specs=[VMEM, VMEM],
+        out_specs=(VMEM, VMEM),
+        scratch_shapes=[kept, kept, sem((2,)), sem((2,)), sem((2, RING, 2)), sem((2, 2))]
+        + [sem((2, 2)), sem((2, 2)), sem((2, 2)), sem((2, RING, 2))],
+        compiler_params=pltpu.CompilerParams(
+            vmem_limit_bytes=24 * 1024 * 1024, collective_id=0, has_side_effects=True
+        ),
+        name="exchange",
+    )(to_left, to_right)
 
 
 VMEM = pl.BlockSpec(memory_space=pltpu.VMEM)
@@ -167,8 +332,6 @@
     py, px = lax.axis_index("py"), lax.axis_index("px")
     height = rows * lax.axis_size("py")
     edge = jnp.stack([RADIUS - py * rows, RADIUS - py * rows + height]).astype(jnp.int32)
-    ring = min(RING, lax.axis_size("px"))
-    turned = jnp.stack([px % ring == 0, px % ring == ring - 1]).astype(jnp.int32)
     bands = row_band(rows), col_band(cols, px * cols, cols * lax.axis_size("px"))
     filtered = []
     for c in range(CHUNKS):
@@ -187,18 +350,17 @@
             cost_estimate=pl.CostEstimate(flops=10**9, bytes_accessed=10**7, transcendentals=0),
             name="rows",
         )(shift, edge, raw, up, down)
-        east, east_far = moved_px(to_left, -1, c % 2 == 0)
-        west, west_far = moved_px(to_right, 1, c % 2 == 0)
+        west, east = exchanged(to_left, to_right)
         filtered.append(
             pl.pallas_call(
                 columns_kernel,
                 out_shape=jax.ShapeDtypeStruct((part * rows, cols), jnp.float32),
-                in_specs=[SMEM, SMEM] + [VMEM] * 7,
+                in_specs=[SMEM] + [VMEM] * 5,
                 out_specs=VMEM,
                 compiler_params=PARAMS,
                 cost_estimate=pl.CostEstimate(flops=10**9, bytes_accessed=10**7, transcendentals=0),
                 name="columns",
-            )(shift, turned, reg, west, west_far, east, east_far, *bands)
+            )(shift, reg, west, east, *bands)
         )
     groups = lax.axis_size("fr")
     me = lax.axis_index("fr")

time: 227 us -> 200 us (0.88)
  the two profiles are of different devices: /device:TPU:29 before, /device:TPU:26 now
where the time goes in v3:
time: 200 us; the launch traced here: 199 us
  Pallas kernels  101 us (50%)
  waiting for transfers between devices  66.8 us (33%)
  starting transfers between devices  23.7 us (12%)
  local copies, waits for them, and re-layouts  6.24 us (3%)
    pallas_call x1, Pallas kernels, exchanged(): pl.pallas_call(exchange_kernel, out_shape=(tile, tile), in_specs=[VMEM, V...  61.8 us
    ppermute x4, waiting for transfers between devices, body(): near = lax.ppermute(send, 'fr', [(i, i ^ 1) for i in range(groups)])  29.2 us
    ppermute x2, waiting for transfers between devices, moved(): return lax.ppermute(cells, axis, pairs)  19.7 us
    ppermute x4, waiting for transfers between devices, body(): far = lax.ppermute(onward, 'fr', [(i, i ^ 2) for i in range(groups)])  17.9 us
    pallas_call x4, Pallas kernels, body(): pl.pallas_call(functools.partial(project_kernel, c * count, rows), out_sh...  15.7 us
    pallas_call x1, Pallas kernels, body(): pl.pallas_call(columns_kernel, out_shape=jax.ShapeDtypeStruct((part * row...  15.6 us
    ppermute x4, starting transfers between devices, body(): near = lax.ppermute(send, 'fr', [(i, i ^ 1) for i in range(groups)])  11.7 us
    pallas_call x1, Pallas kernels, body(): pl.pallas_call(rows_kernel, out_shape=(jax.ShapeDtypeStruct((part, tall,...  8.01 us
  transfers between devices with their start and end apart: 10, of which 8 were waited for; matrix products, arithmetic and copies ran while one was open for 1% of the time, Pallas kernels for 6%

profile of v3, /device:TPU:26, one launch (start us, length us, event | category | flops | bytes accessed | tf_op | source)
XLA Modules:
  0.0 199.4 jit_solution(15531662185583092319)
XLA Ops:
  0.0 0.0 copy-start.2
  0.0 0.0 copy-start.1
  0.0 0.0 copy-start
  0.0 4.3 %fusion.20 = (bf16[160,40,128]{2,1,0:T(8,128)(2,1)}, bf16[160,40,128]{2,1,0:T(8,128)(2,1)}) fusion(bf16[160,64,128]{2,1,0:T(8,128)(2,1)} %raw_ref.1), kind=kLoop, calls=%fused_computation.50 | loop fusion | bytes 6553600 | tf_op jit(solution)/shard_map/slice | solution.py:341
  4.4 1.9 collective-permute-start.1
  6.3 2.4 %collective-permute-start = (bf16[160,40,128]{2,1,0:T(8,128)(2,1)}, bf16[160,40,128]{2,1,0:T(8,128)(2,1)}, u32[]{:S(2)}, u32[]{:S(2)}) collective-permute-start(bf16[160,40,128]{2,1,0:T(8,128)(2,1)} %get-tuple-element.40), channel_id=1, source_target_pairs={{0,16},{16,32},{32,48},{48,64},{64,80},{80,96},{96,112},{1,17},{17... | collective-permute-start | bytes 4915208 | tf_op jit(solution)/shard_map/ppermute | solution.py:135
  8.7 0.0 copy-done.2
  8.7 0.1 copy.13.shift_ref
  8.8 0.0 copy-done.1
  8.8 0.1 copy.11
  9.0 0.1 pad_add_fusion.edge_ref
  9.1 0.2 select_convert_fusion.col_band_ref
  9.3 15.9 %collective-permute-done.1.down_ref = bf16[160,40,128]{2,1,0:T(8,128)(2,1)} collective-permute-done((bf16[160,40,128]{2,1,0:T(8,128)(2,1)}, bf16[160,40,128]{2,1,0:T(8,128)(2,1)}, u32[]{:S(2)}, u32[]{:S(2)}) %collective-permute-start.1) | collective-permute-done | bytes 1638432 | tf_op jit(solution)/shard_map/ppermute | solution.py:135
  25.2 3.8 %collective-permute-done.up_ref = bf16[160,40,128]{2,1,0:T(8,128)(2,1)} collective-permute-done((bf16[160,40,128]{2,1,0:T(8,128)(2,1)}, bf16[160,40,128]{2,1,0:T(8,128)(2,1)}, u32[]{:S(2)}, u32[]{:S(2)}) %collective-permute-start) | collective-permute-done | bytes 1638432 | tf_op jit(solution)/shard_map/ppermute | solution.py:135
  29.0 0.0 copy-done
  29.0 8.0 %rows.1 = (bf16[160,72,128]{2,1,0:T(8,128)(2,1)S(1)}, bf16[54,72,128]{2,1,0:T(8,128)(2,1)S(1)}, bf16[54,72,128]{2,1,0:T(8,128)(2,1)S(1)}) custom-call(s32[160,2]{1,0:T(8,128)S(1)} %copy.13.shift_ref, s32[2]{0:T(128)S(1)} %pad_add_fusion.edge_ref, bf16[160,64,128]{2,1,0:T(8,128)(2,1)S(1)} %copy-done, bf16[160,40,128]{2,1,0:T(8,128)(2,1)} %collective-permute-done.up_ref, ...), custom_call_target="tpu_custom_call" | custom-call | flops 1000000000 | bytes 10000000 | tf_op jit(solution)/shard_map/rows/pallas_call | solution.py:343
  37.0 61.8 %exchange.1 = (bf16[54,72,128]{2,1,0:T(8,128)(2,1)S(1)}, bf16[54,72,128]{2,1,0:T(8,128)(2,1)S(1)}) custom-call(bf16[54,72,128]{2,1,0:T(8,128)(2,1)S(1)} %get-tuple-element.23.to_left, bf16[54,72,128]{2,1,0:T(8,128)(2,1)S(1)} %get-tuple-element.24.to_right), custom_call_target="tpu_custom_call" | custom-call | tf_op jit(solution)/shard_map/exchange/pallas_call | solution.py:308
  98.9 15.6 %columns.1.refs_0_ = f32[10240,128]{1,0:T(8,128)S(1)} custom-call(s32[160,2]{1,0:T(8,128)S(1)} %copy.13.shift_ref, bf16[160,72,128]{2,1,0:T(8,128)(2,1)S(1)} %get-tuple-element.22.reg_ref, bf16[54,72,128]{2,1,0:T(8,128)(2,1)S(1)} %get-tuple-element.25.west_ref, bf16[54,72,128]{2,1,0:T(8,128)(2,1)S(1)} %get-tuple-element.26.east_ref, ...), custom_call_target="tpu_custom_call" | custom-call | flops 1000000000 | bytes 10000000 | tf_op jit(solution)/shard_map/columns/pallas_call | solution.py:355
  114.5 3.9 %project.7 = (bf16[16,64,128]{2,1,0:T(8,128)(2,1)S(1)}, bf16[16,64,128]{2,1,0:T(8,128)(2,1)S(1)}, bf16[2,16,64,128]{3,2,1,0:T(8,128)(2,1)S(1)}) custom-call(bf16[256,160]{1,0:T(8,128)(2,1)S(1)} %pad_maximum_fusion.weight_ref, f32[10240,128]{1,0:T(8,128)S(1)} %columns.1.refs_0_), custom_call_target="tpu_custom_call" | custom-call | flops 1000000000 | bytes 10000000 | tf_op jit(solution)/shard_map/project/pallas_call | solution.py:378
  118.4 1.9 collective-permute-start.8
  120.4 3.9 %project.6 = (bf16[16,64,128]{2,1,0:T(8,128)(2,1)S(1)}, bf16[16,64,128]{2,1,0:T(8,128)(2,1)S(1)}, bf16[2,16,64,128]{3,2,1,0:T(8,128)(2,1)S(1)}) custom-call(bf16[256,160]{1,0:T(8,128)(2,1)S(1)} %pad_maximum_fusion.weight_ref, f32[10240,128]{1,0:T(8,128)S(1)} %columns.1.refs_0_), custom_call_target="tpu_custom_call" | custom-call | flops 1000000000 | bytes 10000000 | tf_op jit(solution)/shard_map/project/pallas_call | solution.py:378
  124.3 3.9 %collective-permute-start.6 = (bf16[2,16,64,128]{3,2,1,0:T(8,128)(2,1)S(1)}, bf16[2,16,64,128]{3,2,1,0:T(8,128)(2,1)S(1)}, u32[]{:S(2)}, u32[]{:S(2)}) collective-permute-start(bf16[2,16,64,128]{3,2,1,0:T(8,128)(2,1)S(1)} %get-tuple-element.34), channel_id=1, source_target_pairs={{0,128},{128,0},{256,384},{384,256},{1,129},{129,1},{257,385},{385... | collective-permute-start | bytes 1572872 | tf_op jit(solution)/shard_map/ppermute | solution.py:387
  128.2 4.0 %project.5 = (bf16[16,64,128]{2,1,0:T(8,128)(2,1)S(1)}, bf16[16,64,128]{2,1,0:T(8,128)(2,1)S(1)}, bf16[2,16,64,128]{3,2,1,0:T(8,128)(2,1)S(1)}) custom-call(bf16[256,160]{1,0:T(8,128)(2,1)S(1)} %pad_maximum_fusion.weight_ref, f32[10240,128]{1,0:T(8,128)S(1)} %columns.1.refs_0_), custom_call_target="tpu_custom_call" | custom-call | flops 1000000000 | bytes 10000000 | tf_op jit(solution)/shard_map/project/pallas_call | solution.py:378
  132.2 1.9 collective-permute-start.4
  134.1 3.9 %project.4 = (bf16[16,64,128]{2,1,0:T(8,128)(2,1)S(1)}, bf16[16,64,128]{2,1,0:T(8,128)(2,1)S(1)}, bf16[2,16,64,128]{3,2,1,0:T(8,128)(2,1)S(1)}) custom-call(bf16[256,160]{1,0:T(8,128)(2,1)S(1)} %pad_maximum_fusion.weight_ref, f32[10240,128]{1,0:T(8,128)S(1)} %columns.1.refs_0_), custom_call_target="tpu_custom_call" | custom-call | flops 1000000000 | bytes 10000000 | tf_op jit(solution)/shard_map/project/pallas_call | solution.py:378
  138.1 3.9 %collective-permute-start.2 = (bf16[2,16,64,128]{3,2,1,0:T(8,128)(2,1)S(1)}, bf16[2,16,64,128]{3,2,1,0:T(8,128)(2,1)S(1)}, u32[]{:S(2)}, u32[]{:S(2)}) collective-permute-start(bf16[2,16,64,128]{3,2,1,0:T(8,128)(2,1)S(1)} %get-tuple-element.28), channel_id=1, source_target_pairs={{0,128},{128,0},{256,384},{384,256},{1,129},{129,1},{257,385},{385... | collective-permute-start | bytes 1572872 | tf_op jit(solution)/shard_map/ppermute | solution.py:387
  142.0 0.0 collective-permute-done.8
  142.0 0.1 fusion
  142.1 1.9 collective-permute-start.9
  144.0 10.8 %collective-permute-done.6 = bf16[2,16,64,128]{3,2,1,0:T(8,128)(2,1)S(1)} collective-permute-done((bf16[2,16,64,128]{3,2,1,0:T(8,128)(2,1)S(1)}, bf16[2,16,64,128]{3,2,1,0:T(8,128)(2,1)S(1)}, u32[]{:S(2)}, u32[]{:S(2)}) %collective-permute-start.6) | collective-permute-done | bytes 524320 | tf_op jit(solution)/shard_map/ppermute | solution.py:387
  154.8 0.1 fusion.3
  154.9 1.9 collective-permute-start.7
  156.8 11.2 %collective-permute-done.4 = bf16[2,16,64,128]{3,2,1,0:T(8,128)(2,1)S(1)} collective-permute-done((bf16[2,16,64,128]{3,2,1,0:T(8,128)(2,1)S(1)}, bf16[2,16,64,128]{3,2,1,0:T(8,128)(2,1)S(1)}, u32[]{:S(2)}, u32[]{:S(2)}) %collective-permute-start.4) | collective-permute-done | bytes 524320 | tf_op jit(solution)/shard_map/ppermute | solution.py:387
  168.0 0.1 fusion.6
  168.0 1.9 collective-permute-start.5
  170.0 7.3 %collective-permute-done.2 = bf16[2,16,64,128]{3,2,1,0:T(8,128)(2,1)S(1)} collective-permute-done((bf16[2,16,64,128]{3,2,1,0:T(8,128)(2,1)S(1)}, bf16[2,16,64,128]{3,2,1,0:T(8,128)(2,1)S(1)}, u32[]{:S(2)}, u32[]{:S(2)}) %collective-permute-start.2) | collective-permute-done | bytes 524320 | tf_op jit(solution)/shard_map/ppermute | solution.py:387
  177.2 0.1 fusion.9
  177.3 1.9 collective-permute-start.3
  179.2 0.0 collective-permute-done.9
  179.2 0.1 fusion.2
  179.4 7.8 %collective-permute-done.7 = bf16[16,64,128]{2,1,0:T(8,128)(2,1)S(1)} collective-permute-done((bf16[16,64,128]{2,1,0:T(8,128)(2,1)S(1)}, bf16[16,64,128]{2,1,0:T(8,128)(2,1)S(1)}, u32[]{:S(2)}, u32[]{:S(2)}) %collective-permute-start.7) | collective-permute-done | bytes 262176 | tf_op jit(solution)/shard_map/ppermute | solution.py:389
  187.1 0.1 fusion.5
  187.3 5.5 %collective-permute-done.5 = bf16[16,64,128]{2,1,0:T(8,128)(2,1)S(1)} collective-permute-done((bf16[16,64,128]{2,1,0:T(8,128)(2,1)S(1)}, bf16[16,64,128]{2,1,0:T(8,128)(2,1)S(1)}, u32[]{:S(2)}, u32[]{:S(2)}) %collective-permute-start.5) | collective-permute-done | bytes 262176 | tf_op jit(solution)/shard_map/ppermute | solution.py:389
  192.8 0.1 fusion.8
  192.9 4.6 %collective-permute-done.3 = bf16[16,64,128]{2,1,0:T(8,128)(2,1)S(1)} collective-permute-done((bf16[16,64,128]{2,1,0:T(8,128)(2,1)S(1)}, bf16[16,64,128]{2,1,0:T(8,128)(2,1)S(1)}, u32[]{:S(2)}, u32[]{:S(2)}) %collective-permute-start.3) | collective-permute-done | bytes 262176 | tf_op jit(solution)/shard_map/ppermute | solution.py:389
  197.5 0.1 fusion.11
  197.6 0.1 maximum_bitcast_fusion
  197.8 1.6 copy.14
  (5 shorter events, 0.1 us)
Async XLA Ops:
  0.0 8.7 %copy-start.2 = (s32[160,2]{0,1:T(2,128)S(1)}, s32[160,2]{0,1:T(2,128)}, u32[]{:S(2)}) copy-start(s32[160,2]{0,1:T(2,128)} %param.4) | copy-start | bytes 3844
  0.0 8.8 %copy-start.1 = (bf16[160,256]{1,0:T(8,128)(2,1)S(1)}, bf16[160,256]{1,0:T(8,128)(2,1)}, u32[]{:S(2)}) copy-start(bf16[160,256]{1,0:T(8,128)(2,1)} %param.5) | copy-start | bytes 245764
  0.0 29.0 %copy-start = (bf16[160,64,128]{2,1,0:T(8,128)(2,1)S(1)}, bf16[160,64,128]{2,1,0:T(8,128)(2,1)}, u32[]{:S(2)}) copy-start(bf16[160,64,128]{2,1,0:T(8,128)(2,1)} %raw_ref.1) | copy-start | bytes 7864324
  4.4 20.8 %collective-permute-start.1 = (bf16[160,40,128]{2,1,0:T(8,128)(2,1)}, bf16[160,40,128]{2,1,0:T(8,128)(2,1)}, u32[]{:S(2)}, u32[]{:S(2)}) collective-permute-start(bf16[160,40,128]{2,1,0:T(8,128)(2,1)} %get-tuple-element.39), channel_id=1, source_target_pairs={{16,0},{32,16},{48,32},{64,48},{80,64},{96,80},{112,96},{17,1},{33... | collective-permute-start | bytes 4915208 | tf_op jit(solution)/shard_map/ppermute | solution.py:135
  6.3 22.8 %collective-permute-start = (bf16[160,40,128]{2,1,0:T(8,128)(2,1)}, bf16[160,40,128]{2,1,0:T(8,128)(2,1)}, u32[]{:S(2)}, u32[]{:S(2)}) collective-permute-start(bf16[160,40,128]{2,1,0:T(8,128)(2,1)} %get-tuple-element.40), channel_id=1, source_target_pairs={{0,16},{16,32},{32,48},{48,64},{64,80},{80,96},{96,112},{1,17},{17... | collective-permute-start | bytes 4915208 | tf_op jit(solution)/shard_map/ppermute | solution.py:135
  118.4 23.6 %collective-permute-start.8 = (bf16[2,16,64,128]{3,2,1,0:T(8,128)(2,1)S(1)}, bf16[2,16,64,128]{3,2,1,0:T(8,128)(2,1)S(1)}, u32[]{:S(2)}, u32[]{:S(2)}) collective-permute-start(bf16[2,16,64,128]{3,2,1,0:T(8,128)(2,1)S(1)} %get-tuple-element.37), channel_id=1, source_target_pairs={{0,128},{128,0},{256,384},{384,256},{1,129},{129,1},{257,385},{385... | collective-permute-start | bytes 1572872 | tf_op jit(solution)/shard_map/ppermute | solution.py:387
  124.3 30.5 %collective-permute-start.6 = (bf16[2,16,64,128]{3,2,1,0:T(8,128)(2,1)S(1)}, bf16[2,16,64,128]{3,2,1,0:T(8,128)(2,1)S(1)}, u32[]{:S(2)}, u32[]{:S(2)}) collective-permute-start(bf16[2,16,64,128]{3,2,1,0:T(8,128)(2,1)S(1)} %get-tuple-element.34), channel_id=1, source_target_pairs={{0,128},{128,0},{256,384},{384,256},{1,129},{129,1},{257,385},{385... | collective-permute-start | bytes 1572872 | tf_op jit(solution)/shard_map/ppermute | solution.py:387
  132.2 35.7 %collective-permute-start.4 = (bf16[2,16,64,128]{3,2,1,0:T(8,128)(2,1)S(1)}, bf16[2,16,64,128]{3,2,1,0:T(8,128)(2,1)S(1)}, u32[]{:S(2)}, u32[]{:S(2)}) collective-permute-start(bf16[2,16,64,128]{3,2,1,0:T(8,128)(2,1)S(1)} %get-tuple-element.31), channel_id=1, source_target_pairs={{0,128},{128,0},{256,384},{384,256},{1,129},{129,1},{257,385},{385... | collective-permute-start | bytes 1572872 | tf_op jit(solution)/shard_map/ppermute | solution.py:387
  138.1 39.2 %collective-permute-start.2 = (bf16[2,16,64,128]{3,2,1,0:T(8,128)(2,1)S(1)}, bf16[2,16,64,128]{3,2,1,0:T(8,128)(2,1)S(1)}, u32[]{:S(2)}, u32[]{:S(2)}) collective-permute-start(bf16[2,16,64,128]{3,2,1,0:T(8,128)(2,1)S(1)} %get-tuple-element.28), channel_id=1, source_target_pairs={{0,128},{128,0},{256,384},{384,256},{1,129},{129,1},{257,385},{385... | collective-permute-start | bytes 1572872 | tf_op jit(solution)/shard_map/ppermute | solution.py:387
  142.1 37.1 %collective-permute-start.9 = (bf16[16,64,128]{2,1,0:T(8,128)(2,1)S(1)}, bf16[16,64,128]{2,1,0:T(8,128)(2,1)S(1)}, u32[]{:S(2)}, u32[]{:S(2)}) collective-permute-start(bf16[16,64,128]{2,1,0:T(8,128)(2,1)S(1)} %fusion), channel_id=1, source_target_pairs={{0,256},{128,384},{256,0},{384,128},{1,257},{129,385},{257,1},{385... | collective-permute-start | bytes 786440 | tf_op jit(solution)/shard_map/ppermute | solution.py:389
  154.9 32.3 %collective-permute-start.7 = (bf16[16,64,128]{2,1,0:T(8,128)(2,1)S(1)}, bf16[16,64,128]{2,1,0:T(8,128)(2,1)S(1)}, u32[]{:S(2)}, u32[]{:S(2)}) collective-permute-start(bf16[16,64,128]{2,1,0:T(8,128)(2,1)S(1)} %fusion.3), channel_id=1, source_target_pairs={{0,256},{128,384},{256,0},{384,128},{1,257},{129,385},{257,1},{385... | collective-permute-start | bytes 786440 | tf_op jit(solution)/shard_map/ppermute | solution.py:389
  168.0 24.7 %collective-permute-start.5 = (bf16[16,64,128]{2,1,0:T(8,128)(2,1)S(1)}, bf16[16,64,128]{2,1,0:T(8,128)(2,1)S(1)}, u32[]{:S(2)}, u32[]{:S(2)}) collective-permute-start(bf16[16,64,128]{2,1,0:T(8,128)(2,1)S(1)} %fusion.6), channel_id=1, source_target_pairs={{0,256},{128,384},{256,0},{384,128},{1,257},{129,385},{257,1},{385... | collective-permute-start | bytes 786440 | tf_op jit(solution)/shard_map/ppermute | solution.py:389
  177.3 20.2 %collective-permute-start.3 = (bf16[16,64,128]{2,1,0:T(8,128)(2,1)S(1)}, bf16[16,64,128]{2,1,0:T(8,128)(2,1)S(1)}, u32[]{:S(2)}, u32[]{:S(2)}) collective-permute-start(bf16[16,64,128]{2,1,0:T(8,128)(2,1)S(1)} %fusion.9), channel_id=1, source_target_pairs={{0,256},{128,384},{256,0},{384,128},{1,257},{129,385},{257,1},{385... | collective-permute-start | bytes 786440 | tf_op jit(solution)/shard_map/ppermute | solution.py:389

commit v4 on v3

--- a/solution.py
+++ b/solution.py
@@ -14,6 +14,7 @@
 SIDE = 40
 RING = 4
 ROW_CHUNKS = 4
+UNROLL = 4
 PACK = 3
 
 
@@ -94,20 +95,23 @@
     *parts, keep_ref, pass_ref, send_ref = refs
     count, comps, lanes = keep_ref.shape
 
-    def one(i, carry):
-        columns = [
-            part[pl.ds(first + i, part.shape[0] // tile_rows, stride=tile_rows), :] for part in parts
-        ]
-        picture = jnp.concatenate(columns, axis=0).astype(jnp.bfloat16)
-        total = jnp.dot(weight_ref[...], picture, preferred_element_type=jnp.float32)
-        total = total.astype(jnp.bfloat16)
-        keep_ref[i] = total[:comps]
-        pass_ref[i] = total[comps : 2 * comps]
-        send_ref[0, i] = total[2 * comps : 3 * comps]
-        send_ref[1, i] = total[3 * comps :]
+    def some(g, carry):
+        for j in range(UNROLL):
+            i = g * UNROLL + j
+            columns = [
+                part[pl.ds(first + i, part.shape[0] // tile_rows, stride=tile_rows), :]
+                for part in parts
+            ]
+            picture = jnp.concatenate(columns, axis=0).astype(jnp.bfloat16)
+            total = jnp.dot(weight_ref[...], picture, preferred_element_type=jnp.float32)
+            total = total.astype(jnp.bfloat16)
+            keep_ref[i] = total[:comps]
+            pass_ref[i] = total[comps : 2 * comps]
+            send_ref[0, i] = total[2 * comps : 3 * comps]
+            send_ref[1, i] = total[3 * comps :]
         return carry
 
-    lax.fori_loop(0, count, one, 0)
+    lax.fori_loop(0, count // UNROLL, some, 0)
 
 
 def tap():
@@ -129,10 +133,81 @@
     return jnp.where(near & there, tap(), 0.0).astype(jnp.bfloat16)
 
 
-def moved(cells, axis, step):
-    count = lax.axis_size(axis)
-    pairs = [(i, i + step) for i in range(count) if 0 <= i + step < count]
-    return lax.ppermute(cells, axis, pairs)
+def sides_kernel(raw, up, down, out_sem, in_sem):
+    rows = raw.shape[1]
+    count = lax.axis_size("py")
+    me = lax.axis_index("py")
+    has_up, has_down = me > 0, me < count - 1
+    barrier = pltpu.get_barrier_semaphore()
+
+    for there, step in ((has_up, -1), (has_down, 1)):
+        @pl.when(there)
+        def _():
+            pl.semaphore_signal(
+                barrier, inc=1, device_id={"py": me + step}, device_id_type=pl.DeviceIdType.MESH
+            )
+
+    both = has_up & has_down
+
+    @pl.when(both)
+    def _():
+        pl.semaphore_wait(barrier, 2)
+
+    @pl.when(jnp.logical_not(both))
+    def _():
+        pl.semaphore_wait(barrier, 1)
+
+    moves = []
+    for d, (sends, gets, step, first, target) in enumerate(
+        ((has_down, has_up, 1, rows - SIDE, up), (has_up, has_down, -1, 0, down))
+    ):
+        def move(d=d, step=step, first=first, target=target):
+            return pltpu.make_async_remote_copy(
+                src_ref=raw.at[:, pl.ds(first, SIDE)],
+                dst_ref=target,
+                send_sem=out_sem.at[d],
+                recv_sem=in_sem.at[d],
+                device_id={"py": me + step},
+                device_id_type=pl.DeviceIdType.MESH,
+            )
+
+        moves.append((sends, gets, target, move))
+
+    for sends, gets, target, move in moves:
+        @pl.when(sends)
+        def _():
+            move().start()
+
+    for sends, gets, target, move in moves:
+        @pl.when(jnp.logical_not(gets))
+        def _():
+            target[...] = jnp.zeros_like(target)
+
+    for sends, gets, target, move in moves:
+        @pl.when(gets)
+        def _():
+            move().wait_recv()
+
+    for sends, gets, target, move in moves:
+        @pl.when(sends)
+        def _():
+            move().wait_send()
+
+
+def sides_of(raw):
+    frames, _, cols = raw.shape
+    side = jax.ShapeDtypeStruct((frames, SIDE, cols), raw.dtype)
+    return pl.pallas_call(
+        sides_kernel,
+        out_shape=(side, side),
+        in_specs=[pl.BlockSpec(memory_space=pl.ANY)],
+        out_specs=(VMEM, VMEM),
+        scratch_shapes=[pltpu.SemaphoreType.DMA((2,)), pltpu.SemaphoreType.DMA((2,))],
+        compiler_params=pltpu.CompilerParams(
+            vmem_limit_bytes=24 * 1024 * 1024, collective_id=1, has_side_effects=True
+        ),
+        name="sides",
+    )(raw)
 
 
 def exchange_kernel(
@@ -143,8 +218,8 @@
     spot, ring = lax.rem(me, RING), lax.div(me, RING)
     rings = count // RING
     packs = to_left.shape[0]
-    cuts = [packs * k // 6 for k in range(7)]
-    lots = [(0, 1), (2,), (3,), (4, 5)]
+    cuts = [packs * k // 12 for k in range(13)]
+    lots = [(0, 1, 2, 3), (4, 5), (6, 7), (8, 9, 10, 11)]
 
     def piece(ref, k):
         return ref.at[pl.ds(cuts[k], cuts[k + 1] - cuts[k])]
@@ -238,25 +313,26 @@
                     for i, k in each(c):
                         spread(c, i, k).start()
 
-        @pl.when(spot != first)
-        def _():
-            plain().start()
-
     for c in range(RING):
-        for target, first, final, onward, arriving, plain, spread, cross, gather in sides:
-            if c != first:
-                @pl.when((spot == c) & onward)
-                def _():
-                    for i, k in each(c):
+        for i, k in each(c):
+            for target, first, final, onward, arriving, plain, spread, cross, gather in sides:
+                if c != first:
+                    @pl.when((spot == c) & onward)
+                    def _():
                         spread(c, i, k).wait_recv()
                         cross(c, i, k).start()
 
+    for target, first, final, onward, arriving, plain, spread, cross, gather in sides:
+        @pl.when(spot != first)
+        def _():
+            plain().start()
+
     for c in range(RING):
-        for target, first, final, onward, arriving, plain, spread, cross, gather in sides:
-            if c != final:
-                @pl.when((spot == c) & arriving)
-                def _():
-                    for i, k in each(c):
+        for i, k in each(c):
+            for target, first, final, onward, arriving, plain, spread, cross, gather in sides:
+                if c != final:
+                    @pl.when((spot == c) & arriving)
+                    def _():
                         cross(c, i, k).wait_recv()
                         gather(c, i, k).start()
 
@@ -303,15 +379,15 @@
 def exchanged(to_left, to_right):
     tile = jax.ShapeDtypeStruct(to_left.shape, to_left.dtype)
     packs = to_left.shape[0]
-    kept = pltpu.VMEM((2, 2, -(-packs // 6)) + to_left.shape[1:], to_left.dtype)
+    kept = pltpu.VMEM((2, 4, -(-packs // 12)) + to_left.shape[1:], to_left.dtype)
     sem = pltpu.SemaphoreType.DMA
     return pl.pallas_call(
         exchange_kernel,
         out_shape=(tile, tile),
         in_specs=[VMEM, VMEM],
         out_specs=(VMEM, VMEM),
-        scratch_shapes=[kept, kept, sem((2,)), sem((2,)), sem((2, RING, 2)), sem((2, 2))]
-        + [sem((2, 2)), sem((2, 2)), sem((2, 2)), sem((2, RING, 2))],
+        scratch_shapes=[kept, kept, sem((2,)), sem((2,)), sem((2, RING, 4)), sem((2, 4))]
+        + [sem((2, 4)), sem((2, 4)), sem((2, 4)), sem((2, RING, 4))],
         compiler_params=pltpu.CompilerParams(
             vmem_limit_bytes=24 * 1024 * 1024, collective_id=0, has_side_effects=True
         ),
@@ -337,8 +413,7 @@
     for c in range(CHUNKS):
         raw = recording[c * part : (c + 1) * part]
         shift = shifts[c * part : (c + 1) * part]
-        up = moved(raw[:, rows - SIDE :], "py", 1)
-        down = moved(raw[:, :SIDE], "py", -1)
+        up, down = sides_of(raw)
         tile = jax.ShapeDtypeStruct((packs, tall, cols), jnp.bfloat16)
         reg, to_left, to_right = pl.pallas_call(
             rows_kernel,

time: 200 us -> 188 us (0.940)
  the two profiles are of different devices: /device:TPU:26 before, /device:TPU:155 now
where the time goes in v4:
time: 188 us; the launch traced here: 187 us
  Pallas kernels  98.5 us (52%)
  waiting for transfers between devices  58.9 us (31%)
  starting transfers between devices  18.3 us (10%)
  local copies, waits for them, and re-layouts  10.4 us (6%)
    pallas_call x1, Pallas kernels, exchanged(): pl.pallas_call(exchange_kernel, out_shape=(tile, tile), in_specs=[VMEM, V...  46.9 us
    ppermute x4, waiting for transfers between devices, body(): near = lax.ppermute(send, 'fr', [(i, i ^ 1) for i in range(groups)])  37.9 us
    pallas_call x1, Pallas kernels, sides_of(): pl.pallas_call(sides_kernel, out_shape=(side, side), in_specs=[pl.BlockSp...  21.7 us
    ppermute x4, waiting for transfers between devices, body(): far = lax.ppermute(onward, 'fr', [(i, i ^ 2) for i in range(groups)])  21 us
    pallas_call x1, Pallas kernels, body(): pl.pallas_call(columns_kernel, out_shape=jax.ShapeDtypeStruct((part * row...  15.6 us
    ppermute x4, starting transfers between devices, body(): near = lax.ppermute(send, 'fr', [(i, i ^ 1) for i in range(groups)])  10.6 us
    unnamed x14, local copies, waits for them, and re-layouts  8.72 us
    pallas_call x1, Pallas kernels, body(): pl.pallas_call(rows_kernel, out_shape=(jax.ShapeDtypeStruct((part, tall,...  7.94 us
  transfers between devices with their start and end apart: 8, of which 5 were waited for; matrix products, arithmetic and copies ran while one was open for 0% of the time, Pallas kernels for 3%

profile of v4, /device:TPU:155, one launch (start us, length us, event | category | flops | bytes accessed | tf_op | source)
XLA Modules:
  0.0 187.5 jit_solution(10946743557888005705)
XLA Ops:
  0.0 0.8 copy.13.shift_ref
  0.8 1.0 copy.11
  1.8 0.0 copy-start
  1.8 1.7 copy-done
  3.6 0.0 copy-start.1
  3.6 21.7 %sides.1 = (bf16[160,40,128]{2,1,0:T(8,128)(2,1)S(1)}, bf16[160,40,128]{2,1,0:T(8,128)(2,1)S(1)}) custom-call(bf16[160,64,128]{2,1,0:T(8,128)(2,1)S(1)} %copy-done), custom_call_target="tpu_custom_call" | custom-call | tf_op jit(solution)/shard_map/sides/pallas_call | solution.py:200
  25.3 0.0 copy-start.2
  25.3 1.2 copy-done.2
  26.5 0.0 copy-start.4
  26.5 1.2 copy-done.4
  27.6 0.1 pad_add_fusion.edge_ref
  27.7 0.0 copy-done.1
  27.7 0.0 copy-start.3
  27.7 1.4 copy-done.3
  29.1 0.0 copy-start.5
  29.1 1.4 copy-done.5
  30.6 7.9 %rows.1 = (bf16[160,72,128]{2,1,0:T(8,128)(2,1)S(1)}, bf16[54,72,128]{2,1,0:T(8,128)(2,1)S(1)}, bf16[54,72,128]{2,1,0:T(8,128)(2,1)S(1)}) custom-call(s32[160,2]{1,0:T(8,128)S(1)} %copy.13.shift_ref, s32[2]{0:T(128)S(1)} %pad_add_fusion.edge_ref, bf16[160,64,128]{2,1,0:T(8,128)(2,1)S(1)} %copy-done.1, bf16[160,40,128]{2,1,0:T(8,128)(2,1)S(1)} %copy-done.3, ...), custom_call_target="tpu_custom_call" | custom-call | flops 1000000000 | bytes 10000000 | tf_op jit(solution)/shard_map/rows/pallas_call | solution.py:418
  38.5 46.9 %exchange.1 = (bf16[54,72,128]{2,1,0:T(8,128)(2,1)S(1)}, bf16[54,72,128]{2,1,0:T(8,128)(2,1)S(1)}) custom-call(bf16[54,72,128]{2,1,0:T(8,128)(2,1)S(1)} %get-tuple-element.27.to_left, bf16[54,72,128]{2,1,0:T(8,128)(2,1)S(1)} %get-tuple-element.28.to_right), custom_call_target="tpu_custom_call" | custom-call | tf_op jit(solution)/shard_map/exchange/pallas_call | solution.py:384
  85.4 0.1 select_convert_fusion.col_band_ref
  85.6 15.6 %columns.1.refs_0_ = f32[10240,128]{1,0:T(8,128)S(1)} custom-call(s32[160,2]{1,0:T(8,128)S(1)} %copy.13.shift_ref, bf16[160,72,128]{2,1,0:T(8,128)(2,1)S(1)} %get-tuple-element.26.reg_ref, bf16[54,72,128]{2,1,0:T(8,128)(2,1)S(1)} %get-tuple-element.29.west_ref, bf16[54,72,128]{2,1,0:T(8,128)(2,1)S(1)} %get-tuple-element.30.east_ref, ...), custom_call_target="tpu_custom_call" | custom-call | flops 1000000000 | bytes 10000000 | tf_op jit(solution)/shard_map/columns/pallas_call | solution.py:430
  101.2 1.6 project.7
  102.8 1.9 %collective-permute-start.6 = (bf16[2,16,64,128]{3,2,1,0:T(8,128)(2,1)S(1)}, bf16[2,16,64,128]{3,2,1,0:T(8,128)(2,1)S(1)}, u32[]{:S(2)}, u32[]{:S(2)}) collective-permute-start(bf16[2,16,64,128]{3,2,1,0:T(8,128)(2,1)S(1)} %get-tuple-element.41), channel_id=1, source_target_pairs={{0,128},{128,0},{256,384},{384,256},{1,129},{129,1},{257,385},{385... | collective-permute-start | bytes 1572872 | tf_op jit(solution)/shard_map/ppermute | solution.py:462
  104.8 1.6 project.6
  106.4 3.4 %collective-permute-start.4 = (bf16[2,16,64,128]{3,2,1,0:T(8,128)(2,1)S(1)}, bf16[2,16,64,128]{3,2,1,0:T(8,128)(2,1)S(1)}, u32[]{:S(2)}, u32[]{:S(2)}) collective-permute-start(bf16[2,16,64,128]{3,2,1,0:T(8,128)(2,1)S(1)} %get-tuple-element.38), channel_id=1, source_target_pairs={{0,128},{128,0},{256,384},{384,256},{1,129},{129,1},{257,385},{385... | collective-permute-start | bytes 1572872 | tf_op jit(solution)/shard_map/ppermute | solution.py:462
  109.7 1.6 project.5
  111.4 1.9 %collective-permute-start.2 = (bf16[2,16,64,128]{3,2,1,0:T(8,128)(2,1)S(1)}, bf16[2,16,64,128]{3,2,1,0:T(8,128)(2,1)S(1)}, u32[]{:S(2)}, u32[]{:S(2)}) collective-permute-start(bf16[2,16,64,128]{3,2,1,0:T(8,128)(2,1)S(1)} %get-tuple-element.35), channel_id=1, source_target_pairs={{0,128},{128,0},{256,384},{384,256},{1,129},{129,1},{257,385},{385... | collective-permute-start | bytes 1572872 | tf_op jit(solution)/shard_map/ppermute | solution.py:462
  113.3 1.6 project.4
  114.9 3.4 %collective-permute-start = (bf16[2,16,64,128]{3,2,1,0:T(8,128)(2,1)S(1)}, bf16[2,16,64,128]{3,2,1,0:T(8,128)(2,1)S(1)}, u32[]{:S(2)}, u32[]{:S(2)}) collective-permute-start(bf16[2,16,64,128]{3,2,1,0:T(8,128)(2,1)S(1)} %get-tuple-element.32), channel_id=1, source_target_pairs={{0,128},{128,0},{256,384},{384,256},{1,129},{129,1},{257,385},{385... | collective-permute-start | bytes 1572872 | tf_op jit(solution)/shard_map/ppermute | solution.py:462
  118.3 0.0 collective-permute-done.6
  118.3 0.1 fusion
  118.4 1.9 %collective-permute-start.7 = (bf16[16,64,128]{2,1,0:T(8,128)(2,1)S(1)}, bf16[16,64,128]{2,1,0:T(8,128)(2,1)S(1)}, u32[]{:S(2)}, u32[]{:S(2)}) collective-permute-start(bf16[16,64,128]{2,1,0:T(8,128)(2,1)S(1)} %fusion), channel_id=1, source_target_pairs={{0,256},{128,384},{256,0},{384,128},{1,257},{129,385},{257,1},{385... | collective-permute-start | bytes 786440 | tf_op jit(solution)/shard_map/ppermute | solution.py:464
  120.3 13.7 %collective-permute-done.4 = bf16[2,16,64,128]{3,2,1,0:T(8,128)(2,1)S(1)} collective-permute-done((bf16[2,16,64,128]{3,2,1,0:T(8,128)(2,1)S(1)}, bf16[2,16,64,128]{3,2,1,0:T(8,128)(2,1)S(1)}, u32[]{:S(2)}, u32[]{:S(2)}) %collective-permute-start.4) | collective-permute-done | bytes 524320 | tf_op jit(solution)/shard_map/ppermute | solution.py:462
  134.0 0.1 fusion.3
  134.1 1.9 %collective-permute-start.5 = (bf16[16,64,128]{2,1,0:T(8,128)(2,1)S(1)}, bf16[16,64,128]{2,1,0:T(8,128)(2,1)S(1)}, u32[]{:S(2)}, u32[]{:S(2)}) collective-permute-start(bf16[16,64,128]{2,1,0:T(8,128)(2,1)S(1)} %fusion.3), channel_id=1, source_target_pairs={{0,256},{128,384},{256,0},{384,128},{1,257},{129,385},{257,1},{385... | collective-permute-start | bytes 786440 | tf_op jit(solution)/shard_map/ppermute | solution.py:464
  136.0 14.8 %collective-permute-done.2 = bf16[2,16,64,128]{3,2,1,0:T(8,128)(2,1)S(1)} collective-permute-done((bf16[2,16,64,128]{3,2,1,0:T(8,128)(2,1)S(1)}, bf16[2,16,64,128]{3,2,1,0:T(8,128)(2,1)S(1)}, u32[]{:S(2)}, u32[]{:S(2)}) %collective-permute-start.2) | collective-permute-done | bytes 524320 | tf_op jit(solution)/shard_map/ppermute | solution.py:462
  150.9 0.1 fusion.6
  150.9 1.9 %collective-permute-start.3 = (bf16[16,64,128]{2,1,0:T(8,128)(2,1)S(1)}, bf16[16,64,128]{2,1,0:T(8,128)(2,1)S(1)}, u32[]{:S(2)}, u32[]{:S(2)}) collective-permute-start(bf16[16,64,128]{2,1,0:T(8,128)(2,1)S(1)} %fusion.6), channel_id=1, source_target_pairs={{0,256},{128,384},{256,0},{384,128},{1,257},{129,385},{257,1},{385... | collective-permute-start | bytes 786440 | tf_op jit(solution)/shard_map/ppermute | solution.py:464
  152.9 9.3 %collective-permute-done = bf16[2,16,64,128]{3,2,1,0:T(8,128)(2,1)S(1)} collective-permute-done((bf16[2,16,64,128]{3,2,1,0:T(8,128)(2,1)S(1)}, bf16[2,16,64,128]{3,2,1,0:T(8,128)(2,1)S(1)}, u32[]{:S(2)}, u32[]{:S(2)}) %collective-permute-start) | collective-permute-done | bytes 524320 | tf_op jit(solution)/shard_map/ppermute | solution.py:462
  162.2 0.1 fusion.9
  162.3 1.9 %collective-permute-start.1 = (bf16[16,64,128]{2,1,0:T(8,128)(2,1)S(1)}, bf16[16,64,128]{2,1,0:T(8,128)(2,1)S(1)}, u32[]{:S(2)}, u32[]{:S(2)}) collective-permute-start(bf16[16,64,128]{2,1,0:T(8,128)(2,1)S(1)} %fusion.9), channel_id=1, source_target_pairs={{0,256},{128,384},{256,0},{384,128},{1,257},{129,385},{257,1},{385... | collective-permute-start | bytes 786440 | tf_op jit(solution)/shard_map/ppermute | solution.py:464
  164.2 0.0 collective-permute-done.7
  164.2 0.1 fusion.2
  164.3 0.0 collective-permute-done.5
  164.3 0.1 fusion.5
  164.5 15.5 %collective-permute-done.3 = bf16[16,64,128]{2,1,0:T(8,128)(2,1)S(1)} collective-permute-done((bf16[16,64,128]{2,1,0:T(8,128)(2,1)S(1)}, bf16[16,64,128]{2,1,0:T(8,128)(2,1)S(1)}, u32[]{:S(2)}, u32[]{:S(2)}) %collective-permute-start.3) | collective-permute-done | bytes 262176 | tf_op jit(solution)/shard_map/ppermute | solution.py:464
  180.0 0.1 fusion.8
  180.1 5.5 %collective-permute-done.1 = bf16[16,64,128]{2,1,0:T(8,128)(2,1)S(1)} collective-permute-done((bf16[16,64,128]{2,1,0:T(8,128)(2,1)S(1)}, bf16[16,64,128]{2,1,0:T(8,128)(2,1)S(1)}, u32[]{:S(2)}, u32[]{:S(2)}) %collective-permute-start.1) | collective-permute-done | bytes 262176 | tf_op jit(solution)/shard_map/ppermute | solution.py:464
  185.6 0.1 fusion.11
  185.7 0.1 maximum_bitcast_fusion
  185.8 1.6 copy.14
  (5 shorter events, 0.1 us)
Async XLA Ops:
  1.8 1.7 copy-start
  3.6 24.1 %copy-start.1 = (bf16[160,64,128]{2,1,0:T(8,128)(2,1)S(1)}, bf16[160,64,128]{2,1,0:T(8,128)(2,1)}, u32[]{:S(2)}) copy-start(bf16[160,64,128]{2,1,0:T(8,128)(2,1)} %raw_ref.1) | copy-start | bytes 7864324
  25.3 1.2 copy-start.2
  26.5 1.2 copy-start.4
  27.7 1.4 copy-start.3
  29.1 1.4 copy-start.5
  102.8 15.4 %collective-permute-start.6 = (bf16[2,16,64,128]{3,2,1,0:T(8,128)(2,1)S(1)}, bf16[2,16,64,128]{3,2,1,0:T(8,128)(2,1)S(1)}, u32[]{:S(2)}, u32[]{:S(2)}) collective-permute-start(bf16[2,16,64,128]{3,2,1,0:T(8,128)(2,1)S(1)} %get-tuple-element.41), channel_id=1, source_target_pairs={{0,128},{128,0},{256,384},{384,256},{1,129},{129,1},{257,385},{385... | collective-permute-start | bytes 1572872 | tf_op jit(solution)/shard_map/ppermute | solution.py:462
  106.4 27.6 %collective-permute-start.4 = (bf16[2,16,64,128]{3,2,1,0:T(8,128)(2,1)S(1)}, bf16[2,16,64,128]{3,2,1,0:T(8,128)(2,1)S(1)}, u32[]{:S(2)}, u32[]{:S(2)}) collective-permute-start(bf16[2,16,64,128]{3,2,1,0:T(8,128)(2,1)S(1)} %get-tuple-element.38), channel_id=1, source_target_pairs={{0,128},{128,0},{256,384},{384,256},{1,129},{129,1},{257,385},{385... | collective-permute-start | bytes 1572872 | tf_op jit(solution)/shard_map/ppermute | solution.py:462
  111.4 39.5 %collective-permute-start.2 = (bf16[2,16,64,128]{3,2,1,0:T(8,128)(2,1)S(1)}, bf16[2,16,64,128]{3,2,1,0:T(8,128)(2,1)S(1)}, u32[]{:S(2)}, u32[]{:S(2)}) collective-permute-start(bf16[2,16,64,128]{3,2,1,0:T(8,128)(2,1)S(1)} %get-tuple-element.35), channel_id=1, source_target_pairs={{0,128},{128,0},{256,384},{384,256},{1,129},{129,1},{257,385},{385... | collective-permute-start | bytes 1572872 | tf_op jit(solution)/shard_map/ppermute | solution.py:462
  114.9 47.3 %collective-permute-start = (bf16[2,16,64,128]{3,2,1,0:T(8,128)(2,1)S(1)}, bf16[2,16,64,128]{3,2,1,0:T(8,128)(2,1)S(1)}, u32[]{:S(2)}, u32[]{:S(2)}) collective-permute-start(bf16[2,16,64,128]{3,2,1,0:T(8,128)(2,1)S(1)} %get-tuple-element.32), channel_id=1, source_target_pairs={{0,128},{128,0},{256,384},{384,256},{1,129},{129,1},{257,385},{385... | collective-permute-start | bytes 1572872 | tf_op jit(solution)/shard_map/ppermute | solution.py:462
  118.4 45.9 %collective-permute-start.7 = (bf16[16,64,128]{2,1,0:T(8,128)(2,1)S(1)}, bf16[16,64,128]{2,1,0:T(8,128)(2,1)S(1)}, u32[]{:S(2)}, u32[]{:S(2)}) collective-permute-start(bf16[16,64,128]{2,1,0:T(8,128)(2,1)S(1)} %fusion), channel_id=1, source_target_pairs={{0,256},{128,384},{256,0},{384,128},{1,257},{129,385},{257,1},{385... | collective-permute-start | bytes 786440 | tf_op jit(solution)/shard_map/ppermute | solution.py:464
  134.1 30.2 %collective-permute-start.5 = (bf16[16,64,128]{2,1,0:T(8,128)(2,1)S(1)}, bf16[16,64,128]{2,1,0:T(8,128)(2,1)S(1)}, u32[]{:S(2)}, u32[]{:S(2)}) collective-permute-start(bf16[16,64,128]{2,1,0:T(8,128)(2,1)S(1)} %fusion.3), channel_id=1, source_target_pairs={{0,256},{128,384},{256,0},{384,128},{1,257},{129,385},{257,1},{385... | collective-permute-start | bytes 786440 | tf_op jit(solution)/shard_map/ppermute | solution.py:464
  150.9 29.0 %collective-permute-start.3 = (bf16[16,64,128]{2,1,0:T(8,128)(2,1)S(1)}, bf16[16,64,128]{2,1,0:T(8,128)(2,1)S(1)}, u32[]{:S(2)}, u32[]{:S(2)}) collective-permute-start(bf16[16,64,128]{2,1,0:T(8,128)(2,1)S(1)} %fusion.6), channel_id=1, source_target_pairs={{0,256},{128,384},{256,0},{384,128},{1,257},{129,385},{257,1},{385... | collective-permute-start | bytes 786440 | tf_op jit(solution)/shard_map/ppermute | solution.py:464
  162.3 23.3 %collective-permute-start.1 = (bf16[16,64,128]{2,1,0:T(8,128)(2,1)S(1)}, bf16[16,64,128]{2,1,0:T(8,128)(2,1)S(1)}, u32[]{:S(2)}, u32[]{:S(2)}) collective-permute-start(bf16[16,64,128]{2,1,0:T(8,128)(2,1)S(1)} %fusion.9), channel_id=1, source_target_pairs={{0,256},{128,384},{256,0},{384,128},{1,257},{129,385},{257,1},{385... | collective-permute-start | bytes 786440 | tf_op jit(solution)/shard_map/ppermute | solution.py:464

commit v5 on v4

--- a/solution.py
+++ b/solution.py
@@ -219,7 +219,7 @@
     rings = count // RING
     packs = to_left.shape[0]
     cuts = [packs * k // 12 for k in range(13)]
-    lots = [(0, 1, 2, 3), (4, 5), (6, 7), (8, 9, 10, 11)]
+    lots = [(0, 1, 2), (3, 4, 5), (6, 7, 8), (9, 10, 11)]
 
     def piece(ref, k):
         return ref.at[pl.ds(cuts[k], cuts[k + 1] - cuts[k])]

time: 188 us -> 193 us (1.027)
  the two profiles are of different devices: /device:TPU:155 before, /device:TPU:130 now
where the time goes in v5:
time: 193 us
  Pallas kernels  107 us (55%)
  waiting for transfers between devices  52.9 us (27%)
  starting transfers between devices  20.8 us (11%)
  local copies, waits for them, and re-layouts  10.4 us (5%)
    pallas_call x1, Pallas kernels, exchanged(): pl.pallas_call(exchange_kernel, out_shape=(tile, tile), in_specs=[VMEM, V...  55.6 us
    ppermute x4, waiting for transfers between devices, body(): near = lax.ppermute(send, 'fr', [(i, i ^ 1) for i in range(groups)])  35.6 us
    pallas_call x1, Pallas kernels, sides_of(): pl.pallas_call(sides_kernel, out_shape=(side, side), in_specs=[pl.BlockSp...  21.4 us
    ppermute x4, waiting for transfers between devices, body(): far = lax.ppermute(onward, 'fr', [(i, i ^ 2) for i in range(groups)])  17.3 us
    pallas_call x1, Pallas kernels, body(): pl.pallas_call(columns_kernel, out_shape=jax.ShapeDtypeStruct((part * row...  15.6 us
    ppermute x4, starting transfers between devices, body(): near = lax.ppermute(send, 'fr', [(i, i ^ 1) for i in range(groups)])  11.7 us
    ppermute x4, starting transfers between devices, body(): far = lax.ppermute(onward, 'fr', [(i, i ^ 2) for i in range(groups)])  9.14 us
    unnamed x14, local copies, waits for them, and re-layouts  8.72 us
  transfers between devices with their start and end apart: 8, of which 6 were waited for; matrix products, arithmetic and copies ran while one was open for 0% of the time, Pallas kernels for 2%

profile of v5, /device:TPU:130, one launch (start us, length us, event | category | flops | bytes accessed | tf_op | source)
XLA Modules:
  0.0 192.5 jit_solution(15867464711607471918)
XLA Ops:
  0.0 0.8 copy.13.shift_ref
  0.8 1.0 copy.11
  1.8 0.0 copy-start
  1.8 1.7 copy-done
  3.6 0.0 copy-start.1
  3.6 21.4 %sides.1 = (bf16[160,40,128]{2,1,0:T(8,128)(2,1)S(1)}, bf16[160,40,128]{2,1,0:T(8,128)(2,1)S(1)}) custom-call(bf16[160,64,128]{2,1,0:T(8,128)(2,1)S(1)} %copy-done), custom_call_target="tpu_custom_call" | custom-call | tf_op jit(solution)/shard_map/sides/pallas_call | solution.py:200
  25.0 0.0 copy-start.2
  25.0 1.2 copy-done.2
  26.2 0.0 copy-start.4
  26.2 1.2 copy-done.4
  27.4 0.1 pad_add_fusion.edge_ref
  27.4 0.0 copy-done.1
  27.4 0.0 copy-start.3
  27.4 1.4 copy-done.3
  28.9 0.0 copy-start.5
  28.9 1.4 copy-done.5
  30.3 8.0 %rows.1 = (bf16[160,72,128]{2,1,0:T(8,128)(2,1)S(1)}, bf16[54,72,128]{2,1,0:T(8,128)(2,1)S(1)}, bf16[54,72,128]{2,1,0:T(8,128)(2,1)S(1)}) custom-call(s32[160,2]{1,0:T(8,128)S(1)} %copy.13.shift_ref, s32[2]{0:T(128)S(1)} %pad_add_fusion.edge_ref, bf16[160,64,128]{2,1,0:T(8,128)(2,1)S(1)} %copy-done.1, bf16[160,40,128]{2,1,0:T(8,128)(2,1)S(1)} %copy-done.3, ...), custom_call_target="tpu_custom_call" | custom-call | flops 1000000000 | bytes 10000000 | tf_op jit(solution)/shard_map/rows/pallas_call | solution.py:418
  38.2 55.6 %exchange.1 = (bf16[54,72,128]{2,1,0:T(8,128)(2,1)S(1)}, bf16[54,72,128]{2,1,0:T(8,128)(2,1)S(1)}) custom-call(bf16[54,72,128]{2,1,0:T(8,128)(2,1)S(1)} %get-tuple-element.27.to_left, bf16[54,72,128]{2,1,0:T(8,128)(2,1)S(1)} %get-tuple-element.28.to_right), custom_call_target="tpu_custom_call" | custom-call | tf_op jit(solution)/shard_map/exchange/pallas_call | solution.py:384
  93.9 0.1 select_convert_fusion.col_band_ref
  94.1 15.6 %columns.1.refs_0_ = f32[10240,128]{1,0:T(8,128)S(1)} custom-call(s32[160,2]{1,0:T(8,128)S(1)} %copy.13.shift_ref, bf16[160,72,128]{2,1,0:T(8,128)(2,1)S(1)} %get-tuple-element.26.reg_ref, bf16[54,72,128]{2,1,0:T(8,128)(2,1)S(1)} %get-tuple-element.29.west_ref, bf16[54,72,128]{2,1,0:T(8,128)(2,1)S(1)} %get-tuple-element.30.east_ref, ...), custom_call_target="tpu_custom_call" | custom-call | flops 1000000000 | bytes 10000000 | tf_op jit(solution)/shard_map/columns/pallas_call | solution.py:430
  109.7 1.6 project.7
  111.3 2.9 %collective-permute-start.6 = (bf16[2,16,64,128]{3,2,1,0:T(8,128)(2,1)S(1)}, bf16[2,16,64,128]{3,2,1,0:T(8,128)(2,1)S(1)}, u32[]{:S(2)}, u32[]{:S(2)}) collective-permute-start(bf16[2,16,64,128]{3,2,1,0:T(8,128)(2,1)S(1)} %get-tuple-element.41), channel_id=1, source_target_pairs={{0,128},{128,0},{256,384},{384,256},{1,129},{129,1},{257,385},{385... | collective-permute-start | bytes 1572872 | tf_op jit(solution)/shard_map/ppermute | solution.py:462
  114.3 1.6 project.6
  115.8 2.9 %collective-permute-start.4 = (bf16[2,16,64,128]{3,2,1,0:T(8,128)(2,1)S(1)}, bf16[2,16,64,128]{3,2,1,0:T(8,128)(2,1)S(1)}, u32[]{:S(2)}, u32[]{:S(2)}) collective-permute-start(bf16[2,16,64,128]{3,2,1,0:T(8,128)(2,1)S(1)} %get-tuple-element.38), channel_id=1, source_target_pairs={{0,128},{128,0},{256,384},{384,256},{1,129},{129,1},{257,385},{385... | collective-permute-start | bytes 1572872 | tf_op jit(solution)/shard_map/ppermute | solution.py:462
  118.8 1.6 project.5
  120.4 3.0 %collective-permute-start.2 = (bf16[2,16,64,128]{3,2,1,0:T(8,128)(2,1)S(1)}, bf16[2,16,64,128]{3,2,1,0:T(8,128)(2,1)S(1)}, u32[]{:S(2)}, u32[]{:S(2)}) collective-permute-start(bf16[2,16,64,128]{3,2,1,0:T(8,128)(2,1)S(1)} %get-tuple-element.35), channel_id=1, source_target_pairs={{0,128},{128,0},{256,384},{384,256},{1,129},{129,1},{257,385},{385... | collective-permute-start | bytes 1572872 | tf_op jit(solution)/shard_map/ppermute | solution.py:462
  123.3 1.6 project.4
  124.9 2.9 %collective-permute-start = (bf16[2,16,64,128]{3,2,1,0:T(8,128)(2,1)S(1)}, bf16[2,16,64,128]{3,2,1,0:T(8,128)(2,1)S(1)}, u32[]{:S(2)}, u32[]{:S(2)}) collective-permute-start(bf16[2,16,64,128]{3,2,1,0:T(8,128)(2,1)S(1)} %get-tuple-element.32), channel_id=1, source_target_pairs={{0,128},{128,0},{256,384},{384,256},{1,129},{129,1},{257,385},{385... | collective-permute-start | bytes 1572872 | tf_op jit(solution)/shard_map/ppermute | solution.py:462
  127.8 0.2 collective-permute-done.6
  128.0 0.1 fusion
  128.1 3.4 %collective-permute-start.7 = (bf16[16,64,128]{2,1,0:T(8,128)(2,1)S(1)}, bf16[16,64,128]{2,1,0:T(8,128)(2,1)S(1)}, u32[]{:S(2)}, u32[]{:S(2)}) collective-permute-start(bf16[16,64,128]{2,1,0:T(8,128)(2,1)S(1)} %fusion), channel_id=1, source_target_pairs={{0,256},{128,384},{256,0},{384,128},{1,257},{129,385},{257,1},{385... | collective-permute-start | bytes 786440 | tf_op jit(solution)/shard_map/ppermute | solution.py:464
  131.5 16.2 %collective-permute-done.4 = bf16[2,16,64,128]{3,2,1,0:T(8,128)(2,1)S(1)} collective-permute-done((bf16[2,16,64,128]{3,2,1,0:T(8,128)(2,1)S(1)}, bf16[2,16,64,128]{3,2,1,0:T(8,128)(2,1)S(1)}, u32[]{:S(2)}, u32[]{:S(2)}) %collective-permute-start.4) | collective-permute-done | bytes 524320 | tf_op jit(solution)/shard_map/ppermute | solution.py:462
  147.7 0.1 fusion.3
  147.7 1.9 collective-permute-start.5
  149.7 13.9 %collective-permute-done.2 = bf16[2,16,64,128]{3,2,1,0:T(8,128)(2,1)S(1)} collective-permute-done((bf16[2,16,64,128]{3,2,1,0:T(8,128)(2,1)S(1)}, bf16[2,16,64,128]{3,2,1,0:T(8,128)(2,1)S(1)}, u32[]{:S(2)}, u32[]{:S(2)}) %collective-permute-start.2) | collective-permute-done | bytes 524320 | tf_op jit(solution)/shard_map/ppermute | solution.py:462
  163.6 0.1 fusion.6
  163.7 1.9 collective-permute-start.3
  165.6 5.3 %collective-permute-done = bf16[2,16,64,128]{3,2,1,0:T(8,128)(2,1)S(1)} collective-permute-done((bf16[2,16,64,128]{3,2,1,0:T(8,128)(2,1)S(1)}, bf16[2,16,64,128]{3,2,1,0:T(8,128)(2,1)S(1)}, u32[]{:S(2)}, u32[]{:S(2)}) %collective-permute-start) | collective-permute-done | bytes 524320 | tf_op jit(solution)/shard_map/ppermute | solution.py:462
  170.9 0.1 fusion.9
  171.0 1.9 collective-permute-start.1
  172.9 0.0 collective-permute-done.7
  172.9 0.1 fusion.2
  173.0 0.0 collective-permute-done.5
  173.0 0.1 fusion.5
  173.2 13.7 %collective-permute-done.3 = bf16[16,64,128]{2,1,0:T(8,128)(2,1)S(1)} collective-permute-done((bf16[16,64,128]{2,1,0:T(8,128)(2,1)S(1)}, bf16[16,64,128]{2,1,0:T(8,128)(2,1)S(1)}, u32[]{:S(2)}, u32[]{:S(2)}) %collective-permute-start.3) | collective-permute-done | bytes 262176 | tf_op jit(solution)/shard_map/ppermute | solution.py:464
  186.9 0.1 fusion.8
  187.0 3.6 %collective-permute-done.1 = bf16[16,64,128]{2,1,0:T(8,128)(2,1)S(1)} collective-permute-done((bf16[16,64,128]{2,1,0:T(8,128)(2,1)S(1)}, bf16[16,64,128]{2,1,0:T(8,128)(2,1)S(1)}, u32[]{:S(2)}, u32[]{:S(2)}) %collective-permute-start.1) | collective-permute-done | bytes 262176 | tf_op jit(solution)/shard_map/ppermute | solution.py:464
  190.6 0.1 fusion.11
  190.7 0.1 maximum_bitcast_fusion
  190.9 1.6 copy.14
  (5 shorter events, 0.1 us)
Async XLA Ops:
  1.8 1.7 copy-start
  3.6 23.9 %copy-start.1 = (bf16[160,64,128]{2,1,0:T(8,128)(2,1)S(1)}, bf16[160,64,128]{2,1,0:T(8,128)(2,1)}, u32[]{:S(2)}) copy-start(bf16[160,64,128]{2,1,0:T(8,128)(2,1)} %raw_ref.1) | copy-start | bytes 7864324
  25.0 1.2 copy-start.2
  26.2 1.2 copy-start.4
  27.4 1.4 copy-start.3
  28.9 1.4 copy-start.5
  111.3 16.7 %collective-permute-start.6 = (bf16[2,16,64,128]{3,2,1,0:T(8,128)(2,1)S(1)}, bf16[2,16,64,128]{3,2,1,0:T(8,128)(2,1)S(1)}, u32[]{:S(2)}, u32[]{:S(2)}) collective-permute-start(bf16[2,16,64,128]{3,2,1,0:T(8,128)(2,1)S(1)} %get-tuple-element.41), channel_id=1, source_target_pairs={{0,128},{128,0},{256,384},{384,256},{1,129},{129,1},{257,385},{385... | collective-permute-start | bytes 1572872 | tf_op jit(solution)/shard_map/ppermute | solution.py:462
  115.8 31.8 %collective-permute-start.4 = (bf16[2,16,64,128]{3,2,1,0:T(8,128)(2,1)S(1)}, bf16[2,16,64,128]{3,2,1,0:T(8,128)(2,1)S(1)}, u32[]{:S(2)}, u32[]{:S(2)}) collective-permute-start(bf16[2,16,64,128]{3,2,1,0:T(8,128)(2,1)S(1)} %get-tuple-element.38), channel_id=1, source_target_pairs={{0,128},{128,0},{256,384},{384,256},{1,129},{129,1},{257,385},{385... | collective-permute-start | bytes 1572872 | tf_op jit(solution)/shard_map/ppermute | solution.py:462
  120.4 43.2 %collective-permute-start.2 = (bf16[2,16,64,128]{3,2,1,0:T(8,128)(2,1)S(1)}, bf16[2,16,64,128]{3,2,1,0:T(8,128)(2,1)S(1)}, u32[]{:S(2)}, u32[]{:S(2)}) collective-permute-start(bf16[2,16,64,128]{3,2,1,0:T(8,128)(2,1)S(1)} %get-tuple-element.35), channel_id=1, source_target_pairs={{0,128},{128,0},{256,384},{384,256},{1,129},{129,1},{257,385},{385... | collective-permute-start | bytes 1572872 | tf_op jit(solution)/shard_map/ppermute | solution.py:462
  124.9 46.0 %collective-permute-start = (bf16[2,16,64,128]{3,2,1,0:T(8,128)(2,1)S(1)}, bf16[2,16,64,128]{3,2,1,0:T(8,128)(2,1)S(1)}, u32[]{:S(2)}, u32[]{:S(2)}) collective-permute-start(bf16[2,16,64,128]{3,2,1,0:T(8,128)(2,1)S(1)} %get-tuple-element.32), channel_id=1, source_target_pairs={{0,128},{128,0},{256,384},{384,256},{1,129},{129,1},{257,385},{385... | collective-permute-start | bytes 1572872 | tf_op jit(solution)/shard_map/ppermute | solution.py:462
  128.1 44.8 %collective-permute-start.7 = (bf16[16,64,128]{2,1,0:T(8,128)(2,1)S(1)}, bf16[16,64,128]{2,1,0:T(8,128)(2,1)S(1)}, u32[]{:S(2)}, u32[]{:S(2)}) collective-permute-start(bf16[16,64,128]{2,1,0:T(8,128)(2,1)S(1)} %fusion), channel_id=1, source_target_pairs={{0,256},{128,384},{256,0},{384,128},{1,257},{129,385},{257,1},{385... | collective-permute-start | bytes 786440 | tf_op jit(solution)/shard_map/ppermute | solution.py:464
  147.7 25.3 %collective-permute-start.5 = (bf16[16,64,128]{2,1,0:T(8,128)(2,1)S(1)}, bf16[16,64,128]{2,1,0:T(8,128)(2,1)S(1)}, u32[]{:S(2)}, u32[]{:S(2)}) collective-permute-start(bf16[16,64,128]{2,1,0:T(8,128)(2,1)S(1)} %fusion.3), channel_id=1, source_target_pairs={{0,256},{128,384},{256,0},{384,128},{1,257},{129,385},{257,1},{385... | collective-permute-start | bytes 786440 | tf_op jit(solution)/shard_map/ppermute | solution.py:464
  163.7 23.2 %collective-permute-start.3 = (bf16[16,64,128]{2,1,0:T(8,128)(2,1)S(1)}, bf16[16,64,128]{2,1,0:T(8,128)(2,1)S(1)}, u32[]{:S(2)}, u32[]{:S(2)}) collective-permute-start(bf16[16,64,128]{2,1,0:T(8,128)(2,1)S(1)} %fusion.6), channel_id=1, source_target_pairs={{0,256},{128,384},{256,0},{384,128},{1,257},{129,385},{257,1},{385... | collective-permute-start | bytes 786440 | tf_op jit(solution)/shard_map/ppermute | solution.py:464
  171.0 19.6 %collective-permute-start.1 = (bf16[16,64,128]{2,1,0:T(8,128)(2,1)S(1)}, bf16[16,64,128]{2,1,0:T(8,128)(2,1)S(1)}, u32[]{:S(2)}, u32[]{:S(2)}) collective-permute-start(bf16[16,64,128]{2,1,0:T(8,128)(2,1)S(1)} %fusion.9), channel_id=1, source_target_pairs={{0,256},{128,384},{256,0},{384,128},{1,257},{129,385},{257,1},{385... | collective-permute-start | bytes 786440 | tf_op jit(solution)/shard_map/ppermute | solution.py:464
